TPU v7x, 512 devices: a whole 4x4x16 slice. The times are simulated.
512 devices in a mesh: mem: 2 (over x_lo), lat: 8 (over x_hi, y), lon: 32 (over z, core).
Axes of the slice: x: 4 (x_hi: 2, x_lo: 2; x = x_hi * 2 + x_lo), y: 4, z: 16, core: 2. Of those that a mesh axis runs over, the one named last changes fastest.
Arguments:
- members: float32 [2, 87, 64, 4096], P('mem', None, 'lat', 'lon'), may hold values from -6 to 6
- target: float32 [87, 64, 4096], P(None, 'lat', 'lon'), may hold values from -6 to 6
Outputs:
- gradient: float32 [2, 87, 64, 4096], P('mem', None, 'lat', 'lon')
- loss: float32 [], replicated
All inputs are finite; a program needn't handle non-finite values.
Results may differ from a plain program's by a relative error of at most 0.0001.
Values sent between devices are 32-bit elements; how exact they have to be, the bound alone decides.
No kernel may reach another device: no remote copies, remote signals or barrier semaphores. Data moves between devices by JAX's collectives and lax.ppermute only.
A program may use at most 64 MiB of HBM per device.

v0:
```python
import jax
import jax.numpy as jnp
from jax import lax
from jax.sharding import PartitionSpec as P

LEVELS = 7


smooth_eps = 0.05


def passed_along(value, axis, by):
    count = lax.axis_size(axis)
    pairs = [(i, i + by) for i in range(count) if 0 <= i + by < count]
    return lax.ppermute(value, axis, pairs)


def from_behind(value, axis, steps):
    count = lax.axis_size(axis)
    pairs = [(source, (source + steps) % count) for source in range(count)]
    return lax.ppermute(value, axis, pairs)


def from_partner(value, axis, stride):
    mask = 2**stride
    pairs = [(source, source ^ mask) for source in range(lax.axis_size(axis))]
    return lax.ppermute(value, axis, pairs)


def soft_abs(values):
    return jnp.sqrt(values * values + smooth_eps * smooth_eps)


def lat_weights(row_count):
    row_index = jnp.arange(row_count, dtype=jnp.float32)
    return jnp.cos((89.875 - 0.25 * row_index) * (jnp.pi / 180.0))


def rows_ahead(values, reach):
    row_count = values.shape[-2]
    axis_count = lax.axis_size("lat")
    hops, remain = divmod(reach, row_count)
    portions = []
    for distance, portion in ((hops, values[..., remain:, :]), (hops + 1, values[..., :remain, :])):
        if portion.shape[-2] == 0:
            continue
        if distance == 0:
            portions.append(portion)
        elif distance >= axis_count:
            portions.append(jnp.zeros_like(portion))
        else:
            portions.append(passed_along(portion, "lat", -distance))
    return jnp.concatenate(portions, axis=-2)


def cols_ahead(values, reach):
    col_count = values.shape[-1]
    axis_count = lax.axis_size("lon")
    hops, remain = divmod(reach, col_count)
    portions = []
    for distance, portion in ((hops, values[..., remain:]), (hops + 1, values[..., :remain])):
        if distance % axis_count == 0:
            portions.append(portion)
        else:
            portions.append(from_behind(portion, "lon", -(distance % axis_count)))
    return jnp.concatenate(portions, axis=-1)


def rows_behind(values, reach):
    row_count = values.shape[-2]
    axis_count = lax.axis_size("lat")
    hops, remain = divmod(reach, row_count)
    portions = []
    for distance, portion in (
        (hops + 1, values[..., row_count - remain :, :]),
        (hops, values[..., : row_count - remain, :]),
    ):
        if portion.shape[-2] == 0:
            continue
        if distance == 0:
            portions.append(portion)
        elif distance >= axis_count:
            portions.append(jnp.zeros_like(portion))
        else:
            portions.append(passed_along(portion, "lat", distance))
    return jnp.concatenate(portions, axis=-2)


def cols_behind(values, reach):
    col_count = values.shape[-1]
    axis_count = lax.axis_size("lon")
    hops, remain = divmod(reach, col_count)
    portions = []
    for distance, portion in (
        (hops + 1, values[..., col_count - remain :]),
        (hops, values[..., : col_count - remain]),
    ):
        if distance % axis_count == 0:
            portions.append(portion)
        else:
            portions.append(from_behind(portion, "lon", distance % axis_count))
    return jnp.concatenate(portions, axis=-1)


def shards(members, target):
    own_field = members[0]
    channels, row_count, col_count = own_field.shape
    nlat_total = row_count * lax.axis_size("lat")
    nlon_total = col_count * lax.axis_size("lon")
    row_start = lax.axis_index("lat") * row_count
    current = lat_weights(nlat_total)
    global_boxes = [current]
    for level in range(LEVELS):
        reach = 2**level
        current = current + jnp.pad(current, (0, reach))[reach : reach + nlat_total]
        global_boxes.append(current)
    own_boxes = [lax.dynamic_slice_in_dim(vector, row_start, row_count) for vector in global_boxes]
    box_totals = [jnp.sum(vector) for vector in global_boxes]
    own_weight = own_boxes[0][:, None]
    weighted = own_weight * (own_field - target)
    partner_field = from_partner(own_field, "mem", 0)
    box_sum = jnp.stack([weighted, own_weight * (partner_field - target)])
    loss_local = jnp.zeros((), jnp.float32)
    cotangents = []
    for scale in range(LEVELS + 1):
        if scale > 0:
            reach = 2 ** (scale - 1)
            box_sum = box_sum + rows_ahead(box_sum, reach)
            box_sum = box_sum + cols_ahead(box_sum, reach)
        lat_box = own_boxes[scale]
        pool_cells = 2.0**scale
        pooled = box_sum / (pool_cells * lat_box)[:, None]
        own_pool = pooled[0]
        partner_pool = pooled[1]
        spread = own_pool - partner_pool
        spread_abs = soft_abs(spread)
        own_abs = soft_abs(own_pool)
        score = 0.5 * (own_abs + soft_abs(partner_pool)) - 0.5 * spread_abs
        loss_local = loss_local + jnp.sum(lat_box[:, None] * score) / (
            channels * nlon_total * box_totals[scale]
        )
        factor = 0.5 * nlat_total / (box_totals[scale] * pool_cells)
        cotangents.append((own_pool / own_abs - spread / spread_abs) * factor)
    loss = lax.psum(loss_local, ("lat", "lon"))
    adjoint = cotangents[LEVELS]
    for level in reversed(range(LEVELS)):
        reach = 2**level
        adjoint = adjoint + cols_behind(adjoint, reach)
        adjoint = adjoint + rows_behind(adjoint, reach)
        adjoint = adjoint + cotangents[level]
    gradient = (own_weight * adjoint)[None]
    return (gradient, loss)


def solution(mesh):
    placed = (P("mem", None, "lat", "lon"), P(None, "lat", "lon"))
    return jax.shard_map(
        shards,
        mesh=mesh,
        in_specs=placed,
        out_specs=(P("mem", None, "lat", "lon"), P()),
        check_vma=False,
    )
```

profile of v0, /device:TPU:6, one launch (start us, length us, event | category | flops | bytes accessed | tf_op | source)
XLA Modules:
  0.0 953.0 jit_solution(11429645059539195271)
XLA Ops:
  5.8 11.7 %collective-permute-done = f32[87,8,128]{0,1,2:T(8,128)S(1)} collective-permute-done((f32[87,8,128]{0,1,2:T(8,128)S(1)}, f32[87,8,128]{0,1,2:T(8,128)S(1)}, u32[]{:S(2)}, u32[]{:S(2)}) %collective-permute-start) | collective-permute-done | bytes 356384 | tf_op jit(solution)/shard_map/ppermute | solution.py:27
  17.8 5.8 collective-permute-start.1
  27.4 7.2 collective-permute-start.2
  37.2 7.7 collective-permute-start.3
  49.0 4.7 collective-permute-start.4
  56.4 8.0 collective-permute-start.5
  65.2 5.9 collective-permute-done.5
  71.4 6.7 collective-permute-start.6
  81.3 7.7 collective-permute-start.7
  89.8 8.0 collective-permute-done.7
  98.4 8.5 collective-permute-start.8
  110.4 3.5 collective-permute-start.9
  114.6 10.3 %collective-permute-done.9 = f32[2,87,8,128]{3,2,1,0:T(8,128)S(1)} collective-permute-done((f32[2,87,8,128]{3,2,1,0:T(8,128)S(1)}, f32[2,87,8,128]{3,2,1,0:T(8,128)S(1)}, u32[]{:S(2)}, u32[]{:S(2)}) %collective-permute-start.9) | collective-permute-done | bytes 712736 | tf_op jit(solution)/shard_map/ppermute | solution.py:15
  125.6 8.1 collective-permute-start.10
  139.4 8.5 collective-permute-done.11
  148.6 7.6 collective-permute-start.12
  165.3 6.0 collective-permute-done.13
  173.0 6.4 collective-permute-done.14
  182.1 5.6 collective-permute-done.15
  189.7 11.0 %collective-permute-done.16 = f32[87,8,128]{0,1,2:T(8,128)S(1)} collective-permute-done((f32[87,8,128]{0,1,2:T(8,128)S(1)}, f32[87,8,128]{0,1,2:T(8,128)S(1)}, u32[]{:S(2)}, u32[]{:S(2)}) %collective-permute-start.16) | collective-permute-done | bytes 356384 | tf_op jit(solution)/shard_map/ppermute | solution.py:15
  202.3 4.9 collective-permute-done.17
  207.2 7.1 collective-permute-start.18
  215.1 8.1 collective-permute-done.18
  224.7 4.5 collective-permute-done.19
  229.3 6.4 collective-permute-start.20
  236.4 9.6 %collective-permute-done.20 = f32[87,8,128]{0,1,2:T(8,128)S(1)} collective-permute-done((f32[87,8,128]{0,1,2:T(8,128)S(1)}, f32[87,8,128]{0,1,2:T(8,128)S(1)}, u32[]{:S(2)}, u32[]{:S(2)}) %collective-permute-start.20) | collective-permute-done | bytes 356384 | tf_op jit(solution)/shard_map/ppermute | solution.py:15
  247.6 4.3 collective-permute-done.21
  254.8 9.1 collective-permute-done.22
  265.7 4.2 collective-permute-done.23
  272.7 7.9 collective-permute-done.24
  282.2 4.2 collective-permute-done.25
  301.2 650.9 %psum.7 = f32[]{:T(128)} all-reduce(f32[]{:T(128)S(6)} %add.337), channel_id=1, replica_groups=mesh['mem'=2,'lat'=8,'lon'=32] {'lat','lon'}, use_global_device_ids=true, to_apply=%region_15.16 | all-reduce | flops 1 | bytes 8 | tf_op jit(solution)/shard_map/psum | solution.py:144
  (134 shorter events, 66.2 us)
Async XLA Ops:
  1.9 15.6 %collective-permute-start = (f32[87,8,128]{0,1,2:T(8,128)S(1)}, f32[87,8,128]{0,1,2:T(8,128)S(1)}, u32[]{:S(2)}, u32[]{:S(2)}) collective-permute-start(f32[87,8,128]{0,1,2:T(8,128)S(1)} %bitcast.144), channel_id=1, source_target_pairs={{0,256},{256,0},{1,257},{257,1},{2,258},{258,2},{3,259},{259,3},{4... | collective-permute-start | bytes 1069064 | tf_op jit(solution)/shard_map/ppermute | solution.py:27
  17.8 8.3 collective-permute-start.1
  27.4 8.6 collective-permute-start.2
  37.2 11.5 %collective-permute-start.3 = (f32[2,87,2,128]{1,2,3,0:T(2,128)S(1)}, f32[2,87,2,128]{1,2,3,0:T(2,128)S(1)}, u32[]{:S(2)}, u32[]{:S(2)}) collective-permute-start(f32[2,87,2,128]{1,2,3,0:T(2,128)S(1)} %slice.256), channel_id=1, source_target_pairs={{32,0},{64,32},{96,64},{128,96},{160,128},{192,160},{224,192},{33,... | collective-permute-start | bytes 534536 | tf_op jit(solution)/shard_map/ppermute | solution.py:15
  49.0 6.1 collective-permute-start.4
  56.4 14.7 %collective-permute-start.5 = (f32[2,87,4,128]{1,2,3,0:T(4,128)S(1)}, f32[2,87,4,128]{1,2,3,0:T(4,128)S(1)}, u32[]{:S(2)}, u32[]{:S(2)}) collective-permute-start(f32[2,87,4,128]{1,2,3,0:T(4,128)S(1)} %get-tuple-element.62), channel_id=1, source_target_pairs={{32,0},{64,32},{96,64},{128,96},{160,128},{192,160},{224,192},{33,... | collective-permute-start | bytes 1069064 | tf_op jit(solution)/shard_map/ppermute | solution.py:15
  71.4 8.3 collective-permute-start.6
  81.3 16.5 %collective-permute-start.7 = (f32[2,87,8,128]{3,2,1,0:T(8,128)S(1)}, f32[2,87,8,128]{3,2,1,0:T(8,128)S(1)}, u32[]{:S(2)}, u32[]{:S(2)}) collective-permute-start(f32[2,87,8,128]{3,2,1,0:T(8,128)S(1)} %copy.19), channel_id=1, source_target_pairs={{32,0},{64,32},{96,64},{128,96},{160,128},{192,160},{224,192},{33,... | collective-permute-start | bytes 2138120 | tf_op jit(solution)/shard_map/ppermute | solution.py:15
  98.4 10.4 %collective-permute-start.8 = (f32[2,87,8,8]{1,3,2,0:T(8,128)S(1)}, f32[2,87,8,8]{1,3,2,0:T(8,128)S(1)}, u32[]{:S(2)}, u32[]{:S(2)}) collective-permute-start(f32[2,87,8,8]{1,3,2,0:T(8,128)S(1)} %copy.21), channel_id=1, source_target_pairs={{0,31},{1,0},{2,1},{3,2},{4,3},{5,4},{6,5},{7,6},{8,7},{9,8},{10,9... | collective-permute-start | bytes 133640 | tf_op jit(solution)/shard_map/ppermute | solution.py:21
  110.4 14.6 %collective-permute-start.9 = (f32[2,87,8,128]{3,2,1,0:T(8,128)S(1)}, f32[2,87,8,128]{3,2,1,0:T(8,128)S(1)}, u32[]{:S(2)}, u32[]{:S(2)}) collective-permute-start(f32[2,87,8,128]{3,2,1,0:T(8,128)S(1)} %copy.23), channel_id=1, source_target_pairs={{64,0},{96,32},{128,64},{160,96},{192,128},{224,160},{65,1},{97,33... | collective-permute-start | bytes 2138120 | tf_op jit(solution)/shard_map/ppermute | solution.py:15
  125.6 10.6 %collective-permute-start.10 = (f32[2,87,8,16]{1,3,2,0:T(8,128)S(1)}, f32[2,87,8,16]{1,3,2,0:T(8,128)S(1)}, u32[]{:S(2)}, u32[]{:S(2)}) collective-permute-start(f32[2,87,8,16]{1,3,2,0:T(8,128)S(1)} %copy.25), channel_id=1, source_target_pairs={{0,31},{1,0},{2,1},{3,2},{4,3},{5,4},{6,5},{7,6},{8,7},{9,8},{10,9... | collective-permute-start | bytes 267272 | tf_op jit(solution)/shard_map/ppermute | solution.py:21
  137.9 10.0 %collective-permute-start.11 = (f32[2,87,8,128]{3,2,1,0:T(8,128)S(1)}, f32[2,87,8,128]{3,2,1,0:T(8,128)S(1)}, u32[]{:S(2)}, u32[]{:S(2)}) collective-permute-start(f32[2,87,8,128]{3,2,1,0:T(8,128)S(1)} %copy.27), channel_id=1, source_target_pairs={{128,0},{160,32},{192,64},{224,96},{129,1},{161,33},{193,65},{225,... | collective-permute-start | bytes 2138120 | tf_op jit(solution)/shard_map/ppermute | solution.py:15
  148.6 11.5 %collective-permute-start.12 = (f32[2,87,8,32]{1,3,2,0:T(8,128)S(1)}, f32[2,87,8,32]{1,3,2,0:T(8,128)S(1)}, u32[]{:S(2)}, u32[]{:S(2)}) collective-permute-start(f32[2,87,8,32]{1,3,2,0:T(8,128)S(1)} %copy.29), channel_id=1, source_target_pairs={{0,31},{1,0},{2,1},{3,2},{4,3},{5,4},{6,5},{7,6},{8,7},{9,8},{10,9... | collective-permute-start | bytes 534536 | tf_op jit(solution)/shard_map/ppermute | solution.py:21
  161.4 9.8 %collective-permute-start.13 = (f32[2,87,8,64]{1,3,2,0:T(8,128)S(1)}, f32[2,87,8,64]{1,3,2,0:T(8,128)S(1)}, u32[]{:S(2)}, u32[]{:S(2)}) collective-permute-start(f32[2,87,8,64]{1,3,2,0:T(8,128)S(1)} %copy.31), channel_id=1, source_target_pairs={{0,31},{1,0},{2,1},{3,2},{4,3},{5,4},{6,5},{7,6},{8,7},{9,8},{10,9... | collective-permute-start | bytes 1069064 | tf_op jit(solution)/shard_map/ppermute | solution.py:21
  172.3 7.2 collective-permute-start.14
  182.0 18.7 %copy-start.5 = (f32[2,87,8,128]{1,2,3,0:T(8,128)S(1)}, f32[2,87,8,128]{1,2,3,0:T(8,128)}, u32[]{:S(2)}) copy-start(f32[2,87,8,128]{1,2,3,0:T(8,128)} %get-tuple-element.34) | copy-start | bytes 2138116
  182.0 5.6 collective-permute-start.15
  187.7 13.0 %collective-permute-start.16 = (f32[87,8,128]{0,1,2:T(8,128)S(1)}, f32[87,8,128]{0,1,2:T(8,128)S(1)}, u32[]{:S(2)}, u32[]{:S(2)}) collective-permute-start(f32[87,8,128]{0,1,2:T(8,128)S(1)} %maximum_add_fusion.11), channel_id=1, source_target_pairs={{0,128},{32,160},{64,192},{96,224},{1,129},{33,161},{65,193},{97,2... | collective-permute-start | bytes 1069064 | tf_op jit(solution)/shard_map/ppermute | solution.py:15
  202.2 21.0 %copy-start.4 = (f32[2,87,8,128]{1,2,3,0:T(8,128)S(1)}, f32[2,87,8,128]{1,2,3,0:T(8,128)}, u32[]{:S(2)}) copy-start(f32[2,87,8,128]{1,2,3,0:T(8,128)} %get-tuple-element.28) | copy-start | bytes 2138116
  202.2 4.9 collective-permute-start.17
  207.2 16.0 %collective-permute-start.18 = (f32[87,8,128]{0,1,2:T(8,128)S(1)}, f32[87,8,128]{0,1,2:T(8,128)S(1)}, u32[]{:S(2)}, u32[]{:S(2)}) collective-permute-start(f32[87,8,128]{0,1,2:T(8,128)S(1)} %maximum_add_fusion.12), channel_id=1, source_target_pairs={{0,64},{32,96},{64,128},{96,160},{128,192},{160,224},{1,65},{33,97... | collective-permute-start | bytes 1069064 | tf_op jit(solution)/shard_map/ppermute | solution.py:15
  224.7 21.4 %copy-start.3 = (f32[2,87,8,128]{1,2,3,0:T(8,128)S(1)}, f32[2,87,8,128]{1,2,3,0:T(8,128)}, u32[]{:S(2)}) copy-start(f32[2,87,8,128]{1,2,3,0:T(8,128)} %get-tuple-element.22) | copy-start | bytes 2138116
  224.7 4.6 collective-permute-start.19
  229.3 16.7 %collective-permute-start.20 = (f32[87,8,128]{0,1,2:T(8,128)S(1)}, f32[87,8,128]{0,1,2:T(8,128)S(1)}, u32[]{:S(2)}, u32[]{:S(2)}) collective-permute-start(f32[87,8,128]{0,1,2:T(8,128)S(1)} %maximum_add_fusion.13), channel_id=1, source_target_pairs={{0,32},{32,64},{64,96},{96,128},{128,160},{160,192},{192,224},{1,3... | collective-permute-start | bytes 1069064 | tf_op jit(solution)/shard_map/ppermute | solution.py:15
  247.6 4.4 collective-permute-start.21
  247.6 16.4 %copy-start.2 = (f32[2,87,8,128]{1,2,3,0:T(8,128)S(1)}, f32[2,87,8,128]{1,2,3,0:T(8,128)}, u32[]{:S(2)}) copy-start(f32[2,87,8,128]{1,2,3,0:T(8,128)} %get-tuple-element.16) | copy-start | bytes 2138116
  252.1 11.9 %collective-permute-start.22 = (f32[87,4,128]{0,1,2:T(4,128)S(1)}, f32[87,4,128]{0,1,2:T(4,128)S(1)}, u32[]{:S(2)}, u32[]{:S(2)}) collective-permute-start(f32[87,4,128]{0,1,2:T(4,128)S(1)} %get-tuple-element.65), channel_id=1, source_target_pairs={{0,32},{32,64},{64,96},{96,128},{128,160},{160,192},{192,224},{1,3... | collective-permute-start | bytes 534536 | tf_op jit(solution)/shard_map/ppermute | solution.py:15
  265.6 4.3 collective-permute-start.23
  270.1 10.5 %collective-permute-start.24 = (f32[87,2,128]{0,1,2:T(2,128)S(1)}, f32[87,2,128]{0,1,2:T(2,128)S(1)}, u32[]{:S(2)}, u32[]{:S(2)}) collective-permute-start(f32[87,2,128]{0,1,2:T(2,128)S(1)} %slice.297), channel_id=1, source_target_pairs={{0,32},{32,64},{64,96},{96,128},{128,160},{160,192},{192,224},{1,3... | collective-permute-start | bytes 267272 | tf_op jit(solution)/shard_map/ppermute | solution.py:15
  282.1 4.2 collective-permute-start.25
  282.2 16.8 %copy-start = (f32[2,87,8,128]{1,2,3,0:T(8,128)S(1)}, f32[2,87,8,128]{1,2,3,0:T(8,128)}, u32[]{:S(2)}) copy-start(f32[2,87,8,128]{1,2,3,0:T(8,128)} %get-tuple-element.57) | copy-start | bytes 2138116
  286.5 12.4 %collective-permute-start.26 = (f32[87,1,128]{0,1,2:T(1,128)S(1)}, f32[87,1,128]{0,1,2:T(1,128)S(1)}, u32[]{:S(2)}, u32[]{:S(2)}) collective-permute-start(f32[87,1,128]{0,1,2:T(1,128)S(1)} %slice.303), channel_id=1, source_target_pairs={{0,32},{32,64},{64,96},{96,128},{128,160},{160,192},{192,224},{1,3... | collective-permute-start | bytes 133640 | tf_op jit(solution)/shard_map/ppermute | solution.py:15
  (3 other events, 25.2 us)
where the time goes:
time: 954 us; the launch traced here: 953 us
  blocking collectives  651 us (68%)
  waiting for transfers between devices  147 us (15%)
  starting transfers between devices  103 us (11%)
  other arithmetic  27.1 us (3%)
  between operations  16.7 us (2%)
    psum x1, blocking collectives, shards(): loss = lax.psum(loss_local, ('lat', 'lon'))  651 us
    ppermute x12, waiting for transfers between devices, passed_along(): return lax.ppermute(value, axis, pairs)  84 us
    ppermute x12, starting transfers between devices, passed_along(): return lax.ppermute(value, axis, pairs)  54.8 us
    ppermute x14, waiting for transfers between devices, from_behind(): return lax.ppermute(value, axis, pairs)  51.2 us
    ppermute x14, starting transfers between devices, from_behind(): return lax.ppermute(value, axis, pairs)  45.9 us
  transfers between devices with their start and end apart: 27, of which 26 were waited for; matrix products, arithmetic and copies ran while one was open for 1% of the time, Pallas kernels for 0%

commit v1 on v0

v1 whole, which is shorter than its diff:
```python
import jax
import jax.numpy as jnp
import numpy as np
from jax import lax
from jax.experimental import pallas as pl
from jax.experimental.pallas import tpu as pltpu
from jax.sharding import Mesh, PartitionSpec as P

LEVELS = 7
EPS = 0.05
PLANE = ("mem", "lat")
LON = ("z", "core")


def box_vectors(row_count):
    row_index = np.arange(row_count, dtype=np.float32)
    degrees = np.float32(89.875) - np.float32(0.25) * row_index
    current = np.cos(degrees * np.float32(np.pi / 180.0)).astype(np.float32)
    boxes = [current]
    for level in range(LEVELS):
        reach = 2**level
        shifted = np.zeros_like(current)
        shifted[: max(row_count - reach, 0)] = current[reach:]
        current = current + shifted
        boxes.append(current)
    return boxes


def neighbour(value, by):
    count = lax.axis_size("z") * lax.axis_size("core")
    pairs = [(i, (i + by) % count) for i in range(count)]
    return lax.ppermute(value, LON, pairs)


def spread(value, axes):
    return lax.all_to_all(value, axes, 0, 0, tiled=True)


def box_kernel(loss_scale, grad_scale, channels, west_ref, own_ref, east_ref, eps_ref, weight_ref, grad_ref, cot_ref):
    peers, share = own_ref.shape[0], own_ref.shape[1]
    bands = peers // 2
    lane = lax.broadcasted_iota(jnp.int32, (8, 128), 1)
    row = lax.broadcasted_iota(jnp.int32, (8, 128), 0)
    zero = jnp.zeros((8, 128), jnp.float32)

    def rows_ahead(field, reach):
        if reach >= 8:
            hop = reach // 8
            return [field[b] + field[b + hop] if b + hop < bands else field[b] for b in range(bands)]
        rolled = [pltpu.roll(tile, 8 - reach, 0) for tile in field] + [zero]
        return [field[b] + jnp.where(row < 8 - reach, rolled[b], rolled[b + 1]) for b in range(bands)]

    def rows_behind(field, reach):
        if reach >= 8:
            hop = reach // 8
            return [field[b] + field[b - hop] if b >= hop else field[b] for b in range(bands)]
        rolled = [pltpu.roll(tile, reach, 0) for tile in field]
        before = [zero] + rolled[:-1]
        return [field[b] + jnp.where(row >= reach, rolled[b], before[b]) for b in range(bands)]

    def cols_ahead(west, own, east, reach, last):
        out = ([], [], [])
        for b in range(bands):
            rw, ro, re = (pltpu.roll(tile, 128 - reach, 1) for tile in (west[b], own[b], east[b]))
            out[0].append(west[b] + jnp.where(lane < 128 - reach, rw, ro))
            out[1].append(own[b] + jnp.where(lane < 128 - reach, ro, re))
            if not last:
                out[2].append(east[b] + re)
        return out

    def cols_behind(west, own, reach, last):
        out = ([], [])
        for b in range(bands):
            rw, ro = pltpu.roll(west[b], reach, 1), pltpu.roll(own[b], reach, 1)
            if not last:
                out[0].append(west[b] + rw)
            out[1].append(own[b] + jnp.where(lane >= reach, ro, rw))
        return out

    def evaluate(scale, first, second, band, side):
        eps = eps_ref[scale, band]
        apart = first - second
        t0, t1, td = first * first + eps, second * second + eps, apart * apart + eps
        r0, r1, rd = lax.rsqrt(t0), lax.rsqrt(t1), lax.rsqrt(td)
        away = apart * rd
        cot_ref[scale, 0, side, band] = (first * r0 - away) * grad_scale[scale]
        cot_ref[scale, 1, side, band] = (second * r1 + away) * grad_scale[scale]
        return t0 * r0 + t1 * r1 - td * rd

    def channel(c, total):
        fields = []
        for m in range(2):
            fields.append(
                [
                    [ref[m * bands + b, c] * weight_ref[b] for b in range(bands)]
                    for ref in (west_ref, own_ref, east_ref)
                ]
            )
        for scale in range(LEVELS + 1):
            if scale:
                reach = 2 ** (scale - 1)
                for m in range(2):
                    if reach < 8 * bands:
                        fields[m] = [rows_ahead(field, reach) for field in fields[m]]
                    fields[m] = cols_ahead(*fields[m], reach, scale == LEVELS)
            part = None
            for side in range(2):
                for b in range(bands):
                    term = evaluate(scale, fields[0][side][b], fields[1][side][b], b, side)
                    part = term if part is None else part + term
            total = total + part * loss_scale[scale]
        for m in range(2):
            adjoint = [[cot_ref[LEVELS, m, side, b] for b in range(bands)] for side in range(2)]
            for level in reversed(range(LEVELS)):
                reach = 2**level
                if reach < 8 * bands:
                    adjoint = [rows_behind(field, reach) for field in adjoint]
                west, own = cols_behind(*adjoint, reach, level == 0)
                if level:
                    west = [west[b] + cot_ref[level, m, 0, b] for b in range(bands)]
                own = [own[b] + cot_ref[level, m, 1, b] for b in range(bands)]
                adjoint = [west, own]
            for b in range(bands):
                grad_ref[m * bands + b, c] = adjoint[1][b] * weight_ref[b]
        return total

    first = (lax.axis_index("mem") * lax.axis_size("lat") + lax.axis_index("lat")) * share
    count = jnp.clip(channels - first, 0, share)
    total = lax.fori_loop(0, count, channel, zero)
    for p in range(peers):
        grad_ref[p, share] = total


def shards(members, target):
    channels, row_count, col_count = target.shape
    bands = lax.axis_size("lat")
    peers = lax.axis_size("mem") * bands
    nlat, nlon = row_count * bands, col_count * lax.axis_size("z") * lax.axis_size("core")
    share = -(-channels // peers)
    boxes = box_vectors(nlat)
    totals = [float(np.sum(vector, dtype=np.float64)) for vector in boxes]
    loss_scale = [0.5 / (2.0**s * channels * nlon * totals[s]) for s in range(LEVELS + 1)]
    grad_scale = [0.5 * nlat / (2.0**s * totals[s]) for s in range(LEVELS + 1)]
    eps = np.stack([(np.float32(2.0**s * EPS) * boxes[s]) ** 2 for s in range(LEVELS + 1)])
    eps = np.broadcast_to(eps.reshape(LEVELS + 1, bands, 8, 1), (LEVELS + 1, bands, 8, 128))
    weight = np.broadcast_to(boxes[0].reshape(bands, 8, 1), (bands, 8, 128))

    apart = jnp.pad(members[0] - target, ((0, peers * share - channels), (0, 0), (0, 0)))
    own = spread(apart, PLANE).reshape(peers, share, row_count, col_count)
    east, west = neighbour(own, -1), neighbour(own, 1)
    vmem = pl.BlockSpec(memory_space=pltpu.VMEM)

    def kernel(*refs):
        box_kernel(loss_scale, grad_scale, channels, *refs)

    grad = pl.pallas_call(
        kernel,
        out_shape=jax.ShapeDtypeStruct((peers, share + 1, row_count, col_count), jnp.float32),
        in_specs=[vmem] * 5,
        out_specs=vmem,
        scratch_shapes=[pltpu.VMEM((LEVELS + 1, 2, 2, bands, 8, 128), jnp.float32)],
        name="boxes",
    )(west, own, east, jnp.asarray(eps), jnp.asarray(weight))
    back = spread(grad, PLANE)
    plane_loss = jnp.sum(back[:, share], axis=0)
    all_loss = spread(jnp.broadcast_to(plane_loss[None], (lax.axis_size("z"), 8, 128)), ("z",))
    gradient = back[:, :share].reshape(1, peers * share, row_count, col_count)[:, :channels]
    return gradient, jnp.sum(all_loss)


def solution(mesh):
    grid = mesh.devices
    fine = Mesh(grid.reshape(*grid.shape[:2], grid.shape[2] // 2, 2), ("mem", "lat", "z", "core"))
    spec = P("mem", None, "lat", LON)
    return jax.shard_map(
        shards,
        mesh=fine,
        in_specs=(spec, P(None, "lat", LON)),
        out_specs=(spec, P()),
        check_vma=False,
    )
```

time: 954 us -> 80.1 us (0.08)
  blocking collectives: 651 us -> 28.9 us
  waiting for transfers between devices: 147 us -> 20.4 us
  starting transfers between devices: 103 us -> 14.9 us
  other arithmetic: 27.1 us -> 1.76 us
  between operations: 16.7 us -> 0.68 us
  Pallas kernels: 0 us -> 9.62 us
    psum x1 -> x0, blocking collectives: 651 us -> none  [shards(): loss = lax.psum(loss_local, ('lat', 'lon'))]
    ppermute x27 -> x2, waiting for transfers between devices: 147 us -> 8.41 us  [neighbour(): return lax.ppermute(value, LON, pairs)]
    ppermute x27 -> x2, starting transfers between devices: 103 us -> 7.29 us  [neighbour(): return lax.ppermute(value, LON, pairs)]
    all_to_all x0 -> x2, blocking collectives: none -> 28.9 us  [spread(): return lax.all_to_all(value, axes, 0, 0, tiled=True)]
    reduce_sum x14 -> x2, other arithmetic: 16.9 us -> 0.63 us  [the longest x1 0.61 us: shards(): return (gradient, jnp.sum(all_loss))]
    all_to_all x0 -> x1, waiting for transfers between devices: none -> 12 us  [spread(): return lax.all_to_all(value, axes, 0, 0, tiled=True)]
    pallas_call x0 -> x1, Pallas kernels: none -> 9.62 us  [shards(): pl.pallas_call(kernel, out_shape=jax.ShapeDtypeStruct((peers, share + 1,...]
  transfers between devices with their start and end apart: 27 -> 3, of which waited for: 26 -> 3; matrix products, arithmetic and copies ran while one was open for 1% -> 1% of each run, Pallas kernels for 0% -> 0%
where the time goes in v1:
time: 80.1 us; the launch traced here: 79.4 us
  blocking collectives  28.9 us (36%)
  waiting for transfers between devices  20.4 us (25%)
  starting transfers between devices  14.9 us (19%)
  Pallas kernels  9.62 us (12%)
  local copies, waits for them, and re-layouts  3.05 us (4%)
  other arithmetic  1.76 us (2%)
    all_to_all x2, blocking collectives, spread(): return lax.all_to_all(value, axes, 0, 0, tiled=True)  28.9 us
    all_to_all x1, waiting for transfers between devices, spread(): return lax.all_to_all(value, axes, 0, 0, tiled=True)  12 us
    pallas_call x1, Pallas kernels, shards(): pl.pallas_call(kernel, out_shape=jax.ShapeDtypeStruct((peers, share + 1,...  9.62 us
    ppermute x2, waiting for transfers between devices, neighbour(): return lax.ppermute(value, LON, pairs)  8.41 us
    all_to_all x1, starting transfers between devices, spread(): return lax.all_to_all(value, axes, 0, 0, tiled=True)  7.62 us
    ppermute x2, starting transfers between devices, neighbour(): return lax.ppermute(value, LON, pairs)  7.29 us
  transfers between devices with their start and end apart: 3, of which 3 were waited for; matrix products, arithmetic and copies ran while one was open for 1% of the time, Pallas kernels for 0%

profile of v1, /device:TPU:6, one launch (start us, length us, event | category | flops | bytes accessed | tf_op | source)
XLA Modules:
  0.0 79.4 jit_solution(14300373176070844421)
XLA Ops:
  0.6 1.1 %bitcast_subtract_fusion = f32[87,8,128]{2,1,0:T(8,128)S(1)} fusion(f32[87,8,128]{2,1,0:T(8,128)} %param.5, f32[1,87,8,128]{3,2,1,0:T(8,128)} %param.4), kind=kLoop, calls=%fused_computation | loop fusion | flops 89088 | bytes 1069056 | tf_op jit(solution)/shard_map/sub | solution.py:148
  1.8 0.0 copy-start.4
  1.8 16.0 %all_to_all.15 = f32[96,8,128]{2,1,0:T(8,128)S(1)} all-to-all(f32[96,8,128]{2,1,0:T(8,128)S(1)} %pad.4), channel_id=1, replica_groups=mesh['mem'=2,'lat'=8,'z'=16,'core'=2] {'mem','lat'}, dimensions={0} | all-to-all | bytes 786432 | tf_op jit(solution)/shard_map/all_to_all | solution.py:36
  17.8 0.0 copy-start
  17.8 0.0 copy-start.3
  17.8 7.3 %collective-permute-start.1 = (f32[16,6,8,128]{3,2,1,0:T(8,128)S(1)}, f32[16,6,8,128]{3,2,1,0:T(8,128)S(1)}, u32[]{:S(2)}, u32[]{:S(2)}) collective-permute-start(f32[16,6,8,128]{3,2,1,0:T(8,128)S(1)} %bitcast.4), channel_id=1, source_target_pairs={{0,31},{1,0},{2,1},{3,2},{4,3},{5,4},{6,5},{7,6},{8,7},{9,8},{10,9... | collective-permute-start | bytes 1179656 | tf_op jit(solution)/shard_map/ppermute | solution.py:32
  25.1 0.0 collective-permute-start
  25.1 5.3 %collective-permute-done.1.refs_2_ = f32[16,6,8,128]{3,2,1,0:T(8,128)S(1)} collective-permute-done((f32[16,6,8,128]{3,2,1,0:T(8,128)S(1)}, f32[16,6,8,128]{3,2,1,0:T(8,128)S(1)}, u32[]{:S(2)}, u32[]{:S(2)}) %collective-permute-start.1) | collective-permute-done | bytes 393248 | tf_op jit(solution)/shard_map/ppermute | solution.py:32
  30.4 0.0 copy-start.1
  30.4 3.1 %collective-permute-done.refs_0_ = f32[16,6,8,128]{3,2,1,0:T(8,128)S(1)} collective-permute-done((f32[16,6,8,128]{3,2,1,0:T(8,128)S(1)}, f32[16,6,8,128]{3,2,1,0:T(8,128)S(1)}, u32[]{:S(2)}, u32[]{:S(2)}) %collective-permute-start) | collective-permute-done | bytes 393248 | tf_op jit(solution)/shard_map/ppermute | solution.py:32
  33.5 0.0 copy-done.4
  33.5 0.0 copy-start.2
  33.5 0.8 jit_solution_.7.refs_4_
  34.3 0.0 copy-done.3
  34.3 0.8 %jit_solution_.6.refs_3_ = f32[8,8,8,128]{3,2,1,0:T(8,128)} broadcast(f32[8,8,8]{2,1,0:T(8,128)S(1)} %copy-done.3), dimensions={0,1,2} | broadcast | bytes 264192 | tf_op jit(solution)
  35.1 0.0 copy-done
  35.1 0.0 copy-done.1
  35.1 0.0 copy-done.2
  35.1 9.6 %boxes.1 = f32[16,7,8,128]{3,2,1,0:T(8,128)} custom-call(f32[16,6,8,128]{3,2,1,0:T(8,128)} %copy-done.2, f32[16,6,8,128]{3,2,1,0:T(8,128)} %bitcast.6, f32[16,6,8,128]{3,2,1,0:T(8,128)} %copy-done.1, f32[8,8,8,128]{3,2,1,0:T(8,128)} %jit_solution_.6.refs_3_, f32[8,8,128]{2,1,0:T(8,128)} %jit_solution_.7.refs_4_), custom_call_target="tpu_custom_call" | custom-call | tf_op jit(solution)/shard_map/boxes/pallas_call | solution.py:156
  44.8 12.9 %all_to_all.16 = f32[16,7,8,128]{3,2,1,0:T(8,128)S(1)} all-to-all(f32[16,7,8,128]{3,2,1,0:T(8,128)} %boxes.1), channel_id=1, replica_groups=mesh['mem'=2,'lat'=8,'z'=16,'core'=2] {'mem','lat'}, dimensions={0} | all-to-all | bytes 917504 | tf_op jit(solution)/shard_map/all_to_all | solution.py:36
  57.7 0.6 broadcast_in_dim.2
  58.3 7.6 %all-to-all-start.2 = ((f32[16,8,128]{2,1,0:T(8,128)}), f32[16,8,128]{2,1,0:T(8,128)S(1)}, u32[]{:S(2)}, u32[]{:S(2)}) async-start(f32[16,8,128]{2,1,0:T(8,128)} %broadcast_in_dim.2), calls=%async_computation.2 | async-start | bytes 131072 | tf_op jit(solution)/shard_map/all_to_all | solution.py:36
  66.0 0.8 slice.13
  66.7 12.0 %all-to-all-done.2 = f32[16,8,128]{2,1,0:T(8,128)S(1)} async-done(((f32[16,8,128]{2,1,0:T(8,128)}), f32[16,8,128]{2,1,0:T(8,128)S(1)}, u32[]{:S(2)}, u32[]{:S(2)}) %all-to-all-start.2) | async-done | bytes 65568 | tf_op jit(solution)/shard_map/all_to_all | solution.py:36
  78.8 0.6 reduce_sum.19
  (3 shorter events, 0.1 us)
Async XLA Ops:
  1.8 31.7 %copy-start.4 = (f32[8,8]{1,0:T(8,128)S(1)}, f32[8,8]{1,0:T(8,128)}, u32[]{:S(2)}) copy-start(f32[8,8]{1,0:T(8,128)} %constant.9.clone) | copy-start | bytes 772
  17.8 17.3 %copy-start = (f32[96,8,128]{2,1,0:T(8,128)}, f32[96,8,128]{2,1,0:T(8,128)S(1)}, u32[]{:S(2)}) copy-start(f32[96,8,128]{2,1,0:T(8,128)S(1)} %all_to_all.15) | copy-start | bytes 1179652
  17.8 16.5 %copy-start.3 = (f32[8,8,8]{2,1,0:T(8,128)S(1)}, f32[8,8,8]{2,1,0:T(8,128)}, u32[]{:S(2)}) copy-start(f32[8,8,8]{2,1,0:T(8,128)} %constant.8.clone) | copy-start | bytes 6148
  17.8 12.6 %collective-permute-start.1 = (f32[16,6,8,128]{3,2,1,0:T(8,128)S(1)}, f32[16,6,8,128]{3,2,1,0:T(8,128)S(1)}, u32[]{:S(2)}, u32[]{:S(2)}) collective-permute-start(f32[16,6,8,128]{3,2,1,0:T(8,128)S(1)} %bitcast.4), channel_id=1, source_target_pairs={{0,31},{1,0},{2,1},{3,2},{4,3},{5,4},{6,5},{7,6},{8,7},{9,8},{10,9... | collective-permute-start | bytes 1179656 | tf_op jit(solution)/shard_map/ppermute | solution.py:32
  25.1 8.4 %collective-permute-start = (f32[16,6,8,128]{3,2,1,0:T(8,128)S(1)}, f32[16,6,8,128]{3,2,1,0:T(8,128)S(1)}, u32[]{:S(2)}, u32[]{:S(2)}) collective-permute-start(f32[16,6,8,128]{3,2,1,0:T(8,128)S(1)} %bitcast.5), channel_id=1, source_target_pairs={{0,1},{1,2},{2,3},{3,4},{4,5},{5,6},{6,7},{7,8},{8,9},{9,10},{10,1... | collective-permute-start | bytes 1179656 | tf_op jit(solution)/shard_map/ppermute | solution.py:32
  30.4 4.7 %copy-start.1 = (f32[16,6,8,128]{3,2,1,0:T(8,128)}, f32[16,6,8,128]{3,2,1,0:T(8,128)S(1)}, u32[]{:S(2)}) copy-start(f32[16,6,8,128]{3,2,1,0:T(8,128)S(1)} %collective-permute-done.1.refs_2_) | copy-start | bytes 1179652
  33.5 1.6 %copy-start.2 = (f32[16,6,8,128]{3,2,1,0:T(8,128)}, f32[16,6,8,128]{3,2,1,0:T(8,128)S(1)}, u32[]{:S(2)}) copy-start(f32[16,6,8,128]{3,2,1,0:T(8,128)S(1)} %collective-permute-done.refs_0_) | copy-start | bytes 1179652
  58.3 20.5 %all-to-all-start.2 = ((f32[16,8,128]{2,1,0:T(8,128)}), f32[16,8,128]{2,1,0:T(8,128)S(1)}, u32[]{:S(2)}, u32[]{:S(2)}) async-start(f32[16,8,128]{2,1,0:T(8,128)} %broadcast_in_dim.2), calls=%async_computation.2 | async-start | bytes 131072 | tf_op jit(solution)/shard_map/all_to_all | solution.py:36

commit v2 on v1

--- a/solution.py
+++ b/solution.py
@@ -1,3 +1,5 @@
+import functools
+
 import jax
 import jax.numpy as jnp
 import numpy as np
@@ -8,6 +10,7 @@
 
 LEVELS = 7
 EPS = 0.05
+GROUPS = (3, 3)
 PLANE = ("mem", "lat")
 LON = ("z", "core")
 
@@ -36,9 +39,15 @@
     return lax.all_to_all(value, axes, 0, 0, tiled=True)
 
 
-def box_kernel(loss_scale, grad_scale, channels, west_ref, own_ref, east_ref, eps_ref, weight_ref, grad_ref, cot_ref):
-    peers, share = own_ref.shape[0], own_ref.shape[1]
+def box_kernel(loss_scale, grad_scale, channels, start, final, west_ref, own_ref, east_ref, table_ref, *refs):
+    grad_ref, eps_ref, weight_ref, cot_ref = refs[-4:]
+    peers, share, group = own_ref.shape[0], own_ref.shape[1], west_ref.shape[1]
     bands = peers // 2
+    for b in range(bands):
+        table = table_ref[b]
+        for scale in range(LEVELS + 1):
+            eps_ref[scale, b] = jnp.broadcast_to(table[:, scale : scale + 1], (8, 128))
+        weight_ref[b] = jnp.broadcast_to(table[:, LEVELS + 1 : LEVELS + 2], (8, 128))
     lane = lax.broadcasted_iota(jnp.int32, (8, 128), 1)
     row = lax.broadcasted_iota(jnp.int32, (8, 128), 0)
     zero = jnp.zeros((8, 128), jnp.float32)
@@ -92,8 +101,8 @@
         for m in range(2):
             fields.append(
                 [
-                    [ref[m * bands + b, c] * weight_ref[b] for b in range(bands)]
-                    for ref in (west_ref, own_ref, east_ref)
+                    [ref[m * bands + b, c + first] * weight_ref[b] for b in range(bands)]
+                    for ref, first in ((west_ref, 0), (own_ref, start), (east_ref, 0))
                 ]
             )
         for scale in range(LEVELS + 1):
@@ -121,13 +130,13 @@
                 own = [own[b] + cot_ref[level, m, 1, b] for b in range(bands)]
                 adjoint = [west, own]
             for b in range(bands):
-                grad_ref[m * bands + b, c] = adjoint[1][b] * weight_ref[b]
+                grad_ref[m * bands + b, c + start] = adjoint[1][b] * weight_ref[b]
         return total
 
-    first = (lax.axis_index("mem") * lax.axis_size("lat") + lax.axis_index("lat")) * share
-    count = jnp.clip(channels - first, 0, share)
-    total = lax.fori_loop(0, count, channel, zero)
-    for p in range(peers):
+    first = (lax.axis_index("mem") * lax.axis_size("lat") + lax.axis_index("lat")) * share + start
+    count = jnp.clip(channels - first, 0, group)
+    total = lax.fori_loop(0, count, channel, zero if start == 0 else refs[0][0, share])
+    for p in range(peers if final else 1):
         grad_ref[p, share] = total
 
 
@@ -141,29 +150,39 @@
     totals = [float(np.sum(vector, dtype=np.float64)) for vector in boxes]
     loss_scale = [0.5 / (2.0**s * channels * nlon * totals[s]) for s in range(LEVELS + 1)]
     grad_scale = [0.5 * nlat / (2.0**s * totals[s]) for s in range(LEVELS + 1)]
-    eps = np.stack([(np.float32(2.0**s * EPS) * boxes[s]) ** 2 for s in range(LEVELS + 1)])
-    eps = np.broadcast_to(eps.reshape(LEVELS + 1, bands, 8, 1), (LEVELS + 1, bands, 8, 128))
-    weight = np.broadcast_to(boxes[0].reshape(bands, 8, 1), (bands, 8, 128))
+    table = np.zeros((bands, 8, 128), np.float32)
+    for s in range(LEVELS + 1):
+        table[:, :, s] = ((np.float32(2.0**s * EPS) * boxes[s]) ** 2).reshape(bands, 8)
+    table[:, :, LEVELS + 1] = boxes[0].reshape(bands, 8)
 
     apart = jnp.pad(members[0] - target, ((0, peers * share - channels), (0, 0), (0, 0)))
     own = spread(apart, PLANE).reshape(peers, share, row_count, col_count)
-    east, west = neighbour(own, -1), neighbour(own, 1)
     vmem = pl.BlockSpec(memory_space=pltpu.VMEM)
-
-    def kernel(*refs):
-        box_kernel(loss_scale, grad_scale, channels, *refs)
-
-    grad = pl.pallas_call(
-        kernel,
-        out_shape=jax.ShapeDtypeStruct((peers, share + 1, row_count, col_count), jnp.float32),
-        in_specs=[vmem] * 5,
-        out_specs=vmem,
-        scratch_shapes=[pltpu.VMEM((LEVELS + 1, 2, 2, bands, 8, 128), jnp.float32)],
-        name="boxes",
-    )(west, own, east, jnp.asarray(eps), jnp.asarray(weight))
+    grad = None
+    halos = []
+    start = 0
+    for size in GROUPS:
+        part = own[:, start : start + size]
+        halos.append((start, size, neighbour(part, 1), neighbour(part, -1)))
+        start += size
+    for start, size, west, east in halos:
+        grad = pl.pallas_call(
+            functools.partial(box_kernel, loss_scale, grad_scale, channels, start, start + size == share),
+            out_shape=jax.ShapeDtypeStruct((peers, share + 1, row_count, col_count), jnp.float32),
+            in_specs=[vmem] * (4 if start == 0 else 5),
+            out_specs=vmem,
+            input_output_aliases={} if start == 0 else {4: 0},
+            scratch_shapes=[
+                pltpu.VMEM((LEVELS + 1, bands, 8, 128), jnp.float32),
+                pltpu.VMEM((bands, 8, 128), jnp.float32),
+                pltpu.VMEM((LEVELS + 1, 2, 2, bands, 8, 128), jnp.float32),
+            ],
+            compiler_params=pltpu.CompilerParams(vmem_limit_bytes=16 << 20),
+            name=f"boxes_{start}",
+        )(west, own, east, jnp.asarray(table), *(() if start == 0 else (grad,)))
     back = spread(grad, PLANE)
-    plane_loss = jnp.sum(back[:, share], axis=0)
-    all_loss = spread(jnp.broadcast_to(plane_loss[None], (lax.axis_size("z"), 8, 128)), ("z",))
+    plane_loss = jnp.sum(back[:, share], axis=(0, 1))
+    all_loss = spread(jnp.broadcast_to(plane_loss, (lax.axis_size("z"), 1, col_count)), ("z",))
     gradient = back[:, :share].reshape(1, peers * share, row_count, col_count)[:, :channels]
     return gradient, jnp.sum(all_loss)
 

time: 80.1 us -> 73.5 us (0.918)
  waiting for transfers between devices: 20.4 us -> 15 us
  starting transfers between devices: 14.9 us -> 17.8 us
  Pallas kernels: 9.62 us -> 7.92 us
  local copies, waits for them, and re-layouts: 3.05 us -> 1.45 us
    ppermute x2 -> x4, waiting for transfers between devices: 8.41 us -> 3.35 us  [neighbour(): return lax.ppermute(value, LON, pairs)]
    ppermute x2 -> x4, starting transfers between devices: 7.29 us -> 10.3 us  [neighbour(): return lax.ppermute(value, LON, pairs)]
    pallas_call x1 -> x2, Pallas kernels: 9.62 us -> 7.92 us  [shards(): pl.pallas_call(functools.partial(box_kernel, loss_scale, grad_scale, chan...]
    another operation x2 -> x0, local copies, waits for them, and re-layouts: 1.59 us -> none
  transfers between devices with their start and end apart: 3 -> 5, of which waited for: 3 -> 3; matrix products, arithmetic and copies ran while one was open for 1% -> 1% of each run, Pallas kernels for 0% -> 5%
where the time goes in v2:
time: 73.5 us; the launch traced here: 73.2 us
  blocking collectives  28.7 us (39%)
  starting transfers between devices  17.8 us (24%)
  waiting for transfers between devices  15 us (20%)
  Pallas kernels  7.92 us (11%)
  other arithmetic  1.76 us (2%)
  local copies, waits for them, and re-layouts  1.45 us (2%)
    all_to_all x2, blocking collectives, spread(): return lax.all_to_all(value, axes, 0, 0, tiled=True)  28.7 us
    all_to_all x1, waiting for transfers between devices, spread(): return lax.all_to_all(value, axes, 0, 0, tiled=True)  11.6 us
    ppermute x4, starting transfers between devices, neighbour(): return lax.ppermute(value, LON, pairs)  10.3 us
    pallas_call x2, Pallas kernels, shards(): pl.pallas_call(functools.partial(box_kernel, loss_scale, grad_scale, chan...  7.92 us
    all_to_all x1, starting transfers between devices, spread(): return lax.all_to_all(value, axes, 0, 0, tiled=True)  7.55 us
    ppermute x4, waiting for transfers between devices, neighbour(): return lax.ppermute(value, LON, pairs)  3.35 us
  transfers between devices with their start and end apart: 5, of which 3 were waited for; matrix products, arithmetic and copies ran while one was open for 1% of the time, Pallas kernels for 5%

profile of v2, /device:TPU:6, one launch (start us, length us, event | category | flops | bytes accessed | tf_op | source)
XLA Modules:
  0.0 73.2 jit_solution(15457304833393830973)
XLA Ops:
  0.6 1.1 %bitcast_subtract_fusion = f32[87,8,128]{2,1,0:T(8,128)S(1)} fusion(f32[87,8,128]{2,1,0:T(8,128)} %param.4, f32[1,87,8,128]{3,2,1,0:T(8,128)} %param.3), kind=kLoop, calls=%fused_computation | loop fusion | flops 89088 | bytes 1069056 | tf_op jit(solution)/shard_map/sub | solution.py:158
  1.8 16.0 %all_to_all.15 = f32[96,8,128]{2,1,0:T(8,128)S(1)} all-to-all(f32[96,8,128]{2,1,0:T(8,128)S(1)} %pad.4), channel_id=1, replica_groups=mesh['mem'=2,'lat'=8,'z'=16,'core'=2] {'mem','lat'}, dimensions={0} | all-to-all | bytes 786432 | tf_op jit(solution)/shard_map/all_to_all | solution.py:39
  17.8 0.0 copy-start
  17.9 7.3 %collective-permute-start.3 = (f32[16,3,8,128]{3,2,1,0:T(8,128)S(1)}, f32[16,3,8,128]{3,2,1,0:T(8,128)S(1)}, u32[]{:S(2)}, u32[]{:S(2)}) collective-permute-start(f32[16,3,8,128]{3,2,1,0:T(8,128)S(1)} %get-tuple-element.2), channel_id=1, source_target_pairs={{0,31},{1,0},{2,1},{3,2},{4,3},{5,4},{6,5},{7,6},{8,7},{9,8},{10,9... | collective-permute-start | bytes 589832 | tf_op jit(solution)/shard_map/ppermute | solution.py:35
  25.1 0.0 collective-permute-start.2
  25.2 3.0 %collective-permute-start.1 = (f32[16,3,8,128]{3,2,1,0:T(8,128)S(1)}, f32[16,3,8,128]{3,2,1,0:T(8,128)S(1)}, u32[]{:S(2)}, u32[]{:S(2)}) collective-permute-start(f32[16,3,8,128]{3,2,1,0:T(8,128)S(1)} %get-tuple-element.3), channel_id=1, source_target_pairs={{0,31},{1,0},{2,1},{3,2},{4,3},{5,4},{6,5},{7,6},{8,7},{9,8},{10,9... | collective-permute-start | bytes 589832 | tf_op jit(solution)/shard_map/ppermute | solution.py:35
  28.1 0.0 collective-permute-start
  28.1 0.2 collective-permute-done.3.east_ref
  28.3 3.1 %collective-permute-done.2.west_ref = f32[16,3,8,128]{3,2,1,0:T(8,128)S(1)} collective-permute-done((f32[16,3,8,128]{3,2,1,0:T(8,128)S(1)}, f32[16,3,8,128]{3,2,1,0:T(8,128)S(1)}, u32[]{:S(2)}, u32[]{:S(2)}) %collective-permute-start.2) | collective-permute-done | bytes 196640 | tf_op jit(solution)/shard_map/ppermute | solution.py:35
  31.5 0.0 copy-done
  31.5 4.0 %boxes_0.1.refs_0_ = f32[16,7,8,128]{3,2,1,0:T(8,128)S(1)} custom-call(f32[16,3,8,128]{3,2,1,0:T(8,128)S(1)} %collective-permute-done.2.west_ref, f32[16,6,8,128]{3,2,1,0:T(8,128)S(1)} %bitcast.6, f32[16,3,8,128]{3,2,1,0:T(8,128)S(1)} %collective-permute-done.3.east_ref, f32[8,8,128]{2,1,0:T(8,128)S(1)} %copy-done), custom_call_target="tpu_custom_call" | custom-call | tf_op jit(solution)/shard_map/boxes_0/pallas_call | solution.py:169
  35.4 0.0 collective-permute-done.1.east_ref
  35.4 0.0 collective-permute-done.west_ref
  35.4 4.0 %boxes_3.1 = f32[16,7,8,128]{3,2,1,0:T(8,128)S(1)} custom-call(f32[16,3,8,128]{3,2,1,0:T(8,128)S(1)} %collective-permute-done.west_ref, f32[16,6,8,128]{3,2,1,0:T(8,128)S(1)} %bitcast.7, f32[16,3,8,128]{3,2,1,0:T(8,128)S(1)} %collective-permute-done.1.east_ref, f32[8,8,128]{2,1,0:T(8,128)S(1)} %copy-done, ...), custom_call_target="tpu_custom_call", output_to_operand_aliasing={{}: (4, {})} | custom-call | tf_op jit(solution)/shard_map/boxes_3/pallas_call | solution.py:169
  39.4 12.6 %all_to_all.16 = f32[16,7,8,128]{3,2,1,0:T(8,128)S(1)} all-to-all(f32[16,7,8,128]{3,2,1,0:T(8,128)S(1)} %boxes_3.1), channel_id=1, replica_groups=mesh['mem'=2,'lat'=8,'z'=16,'core'=2] {'mem','lat'}, dimensions={0} | all-to-all | bytes 917504 | tf_op jit(solution)/shard_map/all_to_all | solution.py:39
  52.1 0.6 broadcast_in_dim.3
  52.7 7.6 %all-to-all-start.2 = ((f32[16,1,128]{2,1,0:T(1,128)}), f32[16,1,128]{2,1,0:T(1,128)S(1)}, u32[]{:S(2)}, u32[]{:S(2)}) async-start(f32[16,1,128]{2,1,0:T(1,128)} %broadcast_in_dim.3), calls=%async_computation.2 | async-start | bytes 16384 | tf_op jit(solution)/shard_map/all_to_all | solution.py:39
  60.3 0.8 %slice.23 = f32[1,87,8,128]{3,2,1,0:T(8,128)} slice(f32[1,96,8,128]{3,2,1,0:T(8,128)S(1)} %bitcast.8), slice={[0:1], [0:87], [0:8], [0:128]} | slice | bytes 712704 | tf_op jit(solution)/shard_map/slice | solution.py:186
  61.0 11.6 %all-to-all-done.2 = f32[16,1,128]{2,1,0:T(1,128)S(1)} async-done(((f32[16,1,128]{2,1,0:T(1,128)}), f32[16,1,128]{2,1,0:T(1,128)S(1)}, u32[]{:S(2)}, u32[]{:S(2)}) %all-to-all-start.2) | async-done | bytes 8224 | tf_op jit(solution)/shard_map/all_to_all | solution.py:39
  72.6 0.6 reduce_sum.19
  (4 shorter events, 0.1 us)
Async XLA Ops:
  17.8 13.6 %copy-start = (f32[8,8,128]{2,1,0:T(8,128)S(1)}, f32[8,8,128]{2,1,0:T(8,128)}, u32[]{:S(2)}) copy-start(f32[8,8,128]{2,1,0:T(8,128)} %constant.6.clone.table_ref) | copy-start | bytes 98308
  17.9 10.5 %collective-permute-start.3 = (f32[16,3,8,128]{3,2,1,0:T(8,128)S(1)}, f32[16,3,8,128]{3,2,1,0:T(8,128)S(1)}, u32[]{:S(2)}, u32[]{:S(2)}) collective-permute-start(f32[16,3,8,128]{3,2,1,0:T(8,128)S(1)} %get-tuple-element.2), channel_id=1, source_target_pairs={{0,31},{1,0},{2,1},{3,2},{4,3},{5,4},{6,5},{7,6},{8,7},{9,8},{10,9... | collective-permute-start | bytes 589832 | tf_op jit(solution)/shard_map/ppermute | solution.py:35
  25.1 6.3 %collective-permute-start.2 = (f32[16,3,8,128]{3,2,1,0:T(8,128)S(1)}, f32[16,3,8,128]{3,2,1,0:T(8,128)S(1)}, u32[]{:S(2)}, u32[]{:S(2)}) collective-permute-start(f32[16,3,8,128]{3,2,1,0:T(8,128)S(1)} %get-tuple-element.2), channel_id=1, source_target_pairs={{0,1},{1,2},{2,3},{3,4},{4,5},{5,6},{6,7},{7,8},{8,9},{9,10},{10,1... | collective-permute-start | bytes 589832 | tf_op jit(solution)/shard_map/ppermute | solution.py:35
  25.2 10.3 %collective-permute-start.1 = (f32[16,3,8,128]{3,2,1,0:T(8,128)S(1)}, f32[16,3,8,128]{3,2,1,0:T(8,128)S(1)}, u32[]{:S(2)}, u32[]{:S(2)}) collective-permute-start(f32[16,3,8,128]{3,2,1,0:T(8,128)S(1)} %get-tuple-element.3), channel_id=1, source_target_pairs={{0,31},{1,0},{2,1},{3,2},{4,3},{5,4},{6,5},{7,6},{8,7},{9,8},{10,9... | collective-permute-start | bytes 589832 | tf_op jit(solution)/shard_map/ppermute | solution.py:35
  28.1 7.3 %collective-permute-start = (f32[16,3,8,128]{3,2,1,0:T(8,128)S(1)}, f32[16,3,8,128]{3,2,1,0:T(8,128)S(1)}, u32[]{:S(2)}, u32[]{:S(2)}) collective-permute-start(f32[16,3,8,128]{3,2,1,0:T(8,128)S(1)} %get-tuple-element.3), channel_id=1, source_target_pairs={{0,1},{1,2},{2,3},{3,4},{4,5},{5,6},{6,7},{7,8},{8,9},{9,10},{10,1... | collective-permute-start | bytes 589832 | tf_op jit(solution)/shard_map/ppermute | solution.py:35
  52.7 20.0 %all-to-all-start.2 = ((f32[16,1,128]{2,1,0:T(1,128)}), f32[16,1,128]{2,1,0:T(1,128)S(1)}, u32[]{:S(2)}, u32[]{:S(2)}) async-start(f32[16,1,128]{2,1,0:T(1,128)} %broadcast_in_dim.3), calls=%async_computation.2 | async-start | bytes 16384 | tf_op jit(solution)/shard_map/all_to_all | solution.py:39

commit v3 on v2

--- a/solution.py
+++ b/solution.py
@@ -1,4 +1,5 @@
 import functools
+import math
 
 import jax
 import jax.numpy as jnp
@@ -11,6 +12,8 @@
 LEVELS = 7
 EPS = 0.05
 GROUPS = (3, 3)
+FIRST_PLANE = 14
+FIRST_Z = 8
 PLANE = ("mem", "lat")
 LON = ("z", "core")
 
@@ -35,8 +38,14 @@
     return lax.ppermute(value, LON, pairs)
 
 
-def spread(value, axes):
-    return lax.all_to_all(value, axes, 0, 0, tiled=True)
+def turned(count, first):
+    return [(first + i) % count for i in range(count)]
+
+
+def spread(value, axes, first):
+    order = turned(math.prod(lax.axis_size(axis) for axis in axes), first)
+    axes = axes if len(axes) > 1 else axes[0]
+    return lax.all_to_all(value, axes, 0, 0, axis_index_groups=[order] if first else None, tiled=True)
 
 
 def box_kernel(loss_scale, grad_scale, channels, start, final, west_ref, own_ref, east_ref, table_ref, *refs):
@@ -101,8 +110,8 @@
         for m in range(2):
             fields.append(
                 [
-                    [ref[m * bands + b, c + first] * weight_ref[b] for b in range(bands)]
-                    for ref, first in ((west_ref, 0), (own_ref, start), (east_ref, 0))
+                    [ref[(m * bands + b - FIRST_PLANE) % peers, c + skip] * weight_ref[b] for b in range(bands)]
+                    for ref, skip in ((west_ref, 0), (own_ref, start), (east_ref, 0))
                 ]
             )
         for scale in range(LEVELS + 1):
@@ -130,11 +139,12 @@
                 own = [own[b] + cot_ref[level, m, 1, b] for b in range(bands)]
                 adjoint = [west, own]
             for b in range(bands):
-                grad_ref[m * bands + b, c + start] = adjoint[1][b] * weight_ref[b]
+                grad_ref[(m * bands + b - FIRST_PLANE) % peers, c + start] = adjoint[1][b] * weight_ref[b]
         return total
 
-    first = (lax.axis_index("mem") * lax.axis_size("lat") + lax.axis_index("lat")) * share + start
-    count = jnp.clip(channels - first, 0, group)
+    me = lax.axis_index("mem") * lax.axis_size("lat") + lax.axis_index("lat")
+    place = lax.rem(me + (peers - FIRST_PLANE), peers)
+    count = jnp.clip(channels - place * share - start, 0, group)
     total = lax.fori_loop(0, count, channel, zero if start == 0 else refs[0][0, share])
     for p in range(peers if final else 1):
         grad_ref[p, share] = total
@@ -156,7 +166,7 @@
     table[:, :, LEVELS + 1] = boxes[0].reshape(bands, 8)
 
     apart = jnp.pad(members[0] - target, ((0, peers * share - channels), (0, 0), (0, 0)))
-    own = spread(apart, PLANE).reshape(peers, share, row_count, col_count)
+    own = spread(apart, PLANE, FIRST_PLANE).reshape(peers, share, row_count, col_count)
     vmem = pl.BlockSpec(memory_space=pltpu.VMEM)
     grad = None
     halos = []
@@ -180,9 +190,9 @@
             compiler_params=pltpu.CompilerParams(vmem_limit_bytes=16 << 20),
             name=f"boxes_{start}",
         )(west, own, east, jnp.asarray(table), *(() if start == 0 else (grad,)))
-    back = spread(grad, PLANE)
+    back = spread(grad, PLANE, FIRST_PLANE)
     plane_loss = jnp.sum(back[:, share], axis=(0, 1))
-    all_loss = spread(jnp.broadcast_to(plane_loss, (lax.axis_size("z"), 1, col_count)), ("z",))
+    all_loss = spread(jnp.broadcast_to(plane_loss, (lax.axis_size("z"), 1, col_count)), ("z",), FIRST_Z)
     gradient = back[:, :share].reshape(1, peers * share, row_count, col_count)[:, :channels]
     return gradient, jnp.sum(all_loss)
 

time: 73.5 us -> 67.1 us (0.913)
  waiting for transfers between devices: 15 us -> 5.02 us
  blocking collectives: 28.7 us -> 33.7 us
  Pallas kernels: 7.92 us -> 4.15 us
  starting transfers between devices: 17.8 us -> 19.7 us
    all_to_all x1, waiting for transfers between devices: 11.6 us -> 1.67 us  [spread(): lax.all_to_all(value, axes, 0, 0, axis_index_groups=[order] if first else...]
    all_to_all x2, blocking collectives: 28.7 us -> 33.7 us  [spread(): lax.all_to_all(value, axes, 0, 0, axis_index_groups=[order] if first else...]
    all_to_all x1, starting transfers between devices: 7.55 us -> 12 us  [spread(): lax.all_to_all(value, axes, 0, 0, axis_index_groups=[order] if first else...]
    pallas_call x2, Pallas kernels: 7.92 us -> 4.15 us  [shards(): pl.pallas_call(functools.partial(box_kernel, loss_scale, grad_scale, chan...]
    ppermute x4, starting transfers between devices: 10.3 us -> 7.7 us  [neighbour(): return lax.ppermute(value, LON, pairs)]
  transfers between devices with their start and end apart: 5 -> 5, of which waited for: 3 -> 3; matrix products, arithmetic and copies ran while one was open for 1% -> 1% of each run, Pallas kernels for 5% -> 6%
where the time goes in v3:
time: 67.1 us; the launch traced here: 66.5 us
  blocking collectives  33.7 us (50%)
  starting transfers between devices  19.7 us (29%)
  waiting for transfers between devices  5.02 us (7%)
  Pallas kernels  4.15 us (6%)
  other arithmetic  1.76 us (3%)
  local copies, waits for them, and re-layouts  1.45 us (2%)
  between operations  0.68 us (1%)
    all_to_all x2, blocking collectives, spread(): lax.all_to_all(value, axes, 0, 0, axis_index_groups=[order] if first else...  33.7 us
    all_to_all x1, starting transfers between devices, spread(): lax.all_to_all(value, axes, 0, 0, axis_index_groups=[order] if first else...  12 us
    ppermute x4, starting transfers between devices, neighbour(): return lax.ppermute(value, LON, pairs)  7.7 us
    pallas_call x2, Pallas kernels, shards(): pl.pallas_call(functools.partial(box_kernel, loss_scale, grad_scale, chan...  4.15 us
    ppermute x4, waiting for transfers between devices, neighbour(): return lax.ppermute(value, LON, pairs)  3.35 us
    all_to_all x1, waiting for transfers between devices, spread(): lax.all_to_all(value, axes, 0, 0, axis_index_groups=[order] if first else...  1.67 us
  transfers between devices with their start and end apart: 5, of which 3 were waited for; matrix products, arithmetic and copies ran while one was open for 1% of the time, Pallas kernels for 6%

profile of v3, /device:TPU:6, one launch (start us, length us, event | category | flops | bytes accessed | tf_op | source)
XLA Modules:
  0.0 66.5 jit_solution(8089392346589430032)
XLA Ops:
  0.6 1.1 %bitcast_subtract_fusion = f32[87,8,128]{2,1,0:T(8,128)S(1)} fusion(f32[87,8,128]{2,1,0:T(8,128)} %param.4, f32[1,87,8,128]{3,2,1,0:T(8,128)} %param.3), kind=kLoop, calls=%fused_computation | loop fusion | flops 89088 | bytes 1069056 | tf_op jit(solution)/shard_map/sub | solution.py:168
  1.8 16.7 %all_to_all.15 = f32[96,8,128]{2,1,0:T(8,128)S(1)} all-to-all(f32[96,8,128]{2,1,0:T(8,128)S(1)} %pad.4), channel_id=1, replica_groups={{448,480,0,32,64,96,128,160,192,224,256,288,320,352,384,416},{449,481,1..., dimensions={0} | all-to-all | bytes 786432 | tf_op jit(solution)/shard_map/all_to_all | solution.py:48
  18.5 0.0 copy-start
  18.5 4.7 %collective-permute-start.3 = (f32[16,3,8,128]{3,2,1,0:T(8,128)S(1)}, f32[16,3,8,128]{3,2,1,0:T(8,128)S(1)}, u32[]{:S(2)}, u32[]{:S(2)}) collective-permute-start(f32[16,3,8,128]{3,2,1,0:T(8,128)S(1)} %get-tuple-element.2), channel_id=1, source_target_pairs={{0,31},{1,0},{2,1},{3,2},{4,3},{5,4},{6,5},{7,6},{8,7},{9,8},{10,9... | collective-permute-start | bytes 589832 | tf_op jit(solution)/shard_map/ppermute | solution.py:38
  23.3 0.0 collective-permute-start.2
  23.3 3.0 %collective-permute-start.1 = (f32[16,3,8,128]{3,2,1,0:T(8,128)S(1)}, f32[16,3,8,128]{3,2,1,0:T(8,128)S(1)}, u32[]{:S(2)}, u32[]{:S(2)}) collective-permute-start(f32[16,3,8,128]{3,2,1,0:T(8,128)S(1)} %get-tuple-element.3), channel_id=1, source_target_pairs={{0,31},{1,0},{2,1},{3,2},{4,3},{5,4},{6,5},{7,6},{8,7},{9,8},{10,9... | collective-permute-start | bytes 589832 | tf_op jit(solution)/shard_map/ppermute | solution.py:38
  26.2 0.0 collective-permute-start
  26.2 0.2 collective-permute-done.3.east_ref
  26.5 3.1 %collective-permute-done.2.west_ref = f32[16,3,8,128]{3,2,1,0:T(8,128)S(1)} collective-permute-done((f32[16,3,8,128]{3,2,1,0:T(8,128)S(1)}, f32[16,3,8,128]{3,2,1,0:T(8,128)S(1)}, u32[]{:S(2)}, u32[]{:S(2)}) %collective-permute-start.2) | collective-permute-done | bytes 196640 | tf_op jit(solution)/shard_map/ppermute | solution.py:38
  29.6 0.0 copy-done
  29.6 4.0 %boxes_0.1.refs_0_ = f32[16,7,8,128]{3,2,1,0:T(8,128)S(1)} custom-call(f32[16,3,8,128]{3,2,1,0:T(8,128)S(1)} %collective-permute-done.2.west_ref, f32[16,6,8,128]{3,2,1,0:T(8,128)S(1)} %bitcast.6, f32[16,3,8,128]{3,2,1,0:T(8,128)S(1)} %collective-permute-done.3.east_ref, f32[8,8,128]{2,1,0:T(8,128)S(1)} %copy-done), custom_call_target="tpu_custom_call" | custom-call | tf_op jit(solution)/shard_map/boxes_0/pallas_call | solution.py:179
  33.5 0.0 collective-permute-done.1.east_ref
  33.5 0.0 collective-permute-done.west_ref
  33.6 0.2 boxes_3.1
  33.7 17.0 %all_to_all.16 = f32[16,7,8,128]{3,2,1,0:T(8,128)S(1)} all-to-all(f32[16,7,8,128]{3,2,1,0:T(8,128)S(1)} %boxes_3.1), channel_id=1, replica_groups={{448,480,0,32,64,96,128,160,192,224,256,288,320,352,384,416},{449,481,1..., dimensions={0} | all-to-all | bytes 917504 | tf_op jit(solution)/shard_map/all_to_all | solution.py:48
  50.8 0.6 broadcast_in_dim.3
  51.4 12.0 %all-to-all-start.2 = ((f32[16,1,128]{2,1,0:T(1,128)}), f32[16,1,128]{2,1,0:T(1,128)S(1)}, u32[]{:S(2)}, u32[]{:S(2)}) async-start(f32[16,1,128]{2,1,0:T(1,128)} %broadcast_in_dim.3), calls=%async_computation.2 | async-start | bytes 16384 | tf_op jit(solution)/shard_map/all_to_all | solution.py:48
  63.5 0.8 %slice.23 = f32[1,87,8,128]{3,2,1,0:T(8,128)} slice(f32[1,96,8,128]{3,2,1,0:T(8,128)S(1)} %bitcast.8), slice={[0:1], [0:87], [0:8], [0:128]} | slice | bytes 712704 | tf_op jit(solution)/shard_map/slice | solution.py:196
  64.2 1.7 %all-to-all-done.2 = f32[16,1,128]{2,1,0:T(1,128)S(1)} async-done(((f32[16,1,128]{2,1,0:T(1,128)}), f32[16,1,128]{2,1,0:T(1,128)S(1)}, u32[]{:S(2)}, u32[]{:S(2)}) %all-to-all-start.2) | async-done | bytes 8224 | tf_op jit(solution)/shard_map/all_to_all | solution.py:48
  65.9 0.6 reduce_sum.19
  (4 shorter events, 0.1 us)
Async XLA Ops:
  18.5 11.1 %copy-start = (f32[8,8,128]{2,1,0:T(8,128)S(1)}, f32[8,8,128]{2,1,0:T(8,128)}, u32[]{:S(2)}) copy-start(f32[8,8,128]{2,1,0:T(8,128)} %constant.6.clone.table_ref) | copy-start | bytes 98308
  18.5 7.9 %collective-permute-start.3 = (f32[16,3,8,128]{3,2,1,0:T(8,128)S(1)}, f32[16,3,8,128]{3,2,1,0:T(8,128)S(1)}, u32[]{:S(2)}, u32[]{:S(2)}) collective-permute-start(f32[16,3,8,128]{3,2,1,0:T(8,128)S(1)} %get-tuple-element.2), channel_id=1, source_target_pairs={{0,31},{1,0},{2,1},{3,2},{4,3},{5,4},{6,5},{7,6},{8,7},{9,8},{10,9... | collective-permute-start | bytes 589832 | tf_op jit(solution)/shard_map/ppermute | solution.py:38
  23.3 6.3 %collective-permute-start.2 = (f32[16,3,8,128]{3,2,1,0:T(8,128)S(1)}, f32[16,3,8,128]{3,2,1,0:T(8,128)S(1)}, u32[]{:S(2)}, u32[]{:S(2)}) collective-permute-start(f32[16,3,8,128]{3,2,1,0:T(8,128)S(1)} %get-tuple-element.2), channel_id=1, source_target_pairs={{0,1},{1,2},{2,3},{3,4},{4,5},{5,6},{6,7},{7,8},{8,9},{9,10},{10,1... | collective-permute-start | bytes 589832 | tf_op jit(solution)/shard_map/ppermute | solution.py:38
  23.3 10.3 %collective-permute-start.1 = (f32[16,3,8,128]{3,2,1,0:T(8,128)S(1)}, f32[16,3,8,128]{3,2,1,0:T(8,128)S(1)}, u32[]{:S(2)}, u32[]{:S(2)}) collective-permute-start(f32[16,3,8,128]{3,2,1,0:T(8,128)S(1)} %get-tuple-element.3), channel_id=1, source_target_pairs={{0,31},{1,0},{2,1},{3,2},{4,3},{5,4},{6,5},{7,6},{8,7},{9,8},{10,9... | collective-permute-start | bytes 589832 | tf_op jit(solution)/shard_map/ppermute | solution.py:38
  26.2 7.3 %collective-permute-start = (f32[16,3,8,128]{3,2,1,0:T(8,128)S(1)}, f32[16,3,8,128]{3,2,1,0:T(8,128)S(1)}, u32[]{:S(2)}, u32[]{:S(2)}) collective-permute-start(f32[16,3,8,128]{3,2,1,0:T(8,128)S(1)} %get-tuple-element.3), channel_id=1, source_target_pairs={{0,1},{1,2},{2,3},{3,4},{4,5},{5,6},{6,7},{7,8},{8,9},{9,10},{10,1... | collective-permute-start | bytes 589832 | tf_op jit(solution)/shard_map/ppermute | solution.py:38
  51.4 14.5 %all-to-all-start.2 = ((f32[16,1,128]{2,1,0:T(1,128)}), f32[16,1,128]{2,1,0:T(1,128)S(1)}, u32[]{:S(2)}, u32[]{:S(2)}) async-start(f32[16,1,128]{2,1,0:T(1,128)} %broadcast_in_dim.3), calls=%async_computation.2 | async-start | bytes 16384 | tf_op jit(solution)/shard_map/all_to_all | solution.py:48

commit v4 on v3

--- a/solution.py
+++ b/solution.py
@@ -49,7 +49,8 @@
 
 
 def box_kernel(loss_scale, grad_scale, channels, start, final, west_ref, own_ref, east_ref, table_ref, *refs):
-    grad_ref, eps_ref, weight_ref, cot_ref = refs[-4:]
+    eps_ref, weight_ref, cot_ref = refs[-3:]
+    grad_ref, term_ref = refs[-5:-3] if final else (refs[-4], None)
     peers, share, group = own_ref.shape[0], own_ref.shape[1], west_ref.shape[1]
     bands = peers // 2
     for b in range(bands):
@@ -146,8 +147,40 @@
     place = lax.rem(me + (peers - FIRST_PLANE), peers)
     count = jnp.clip(channels - place * share - start, 0, group)
     total = lax.fori_loop(0, count, channel, zero if start == 0 else refs[0][0, share])
-    for p in range(peers if final else 1):
-        grad_ref[p, share] = total
+    if final:
+        term_ref[...] = jnp.broadcast_to(jnp.sum(total, axis=0).reshape(1, 1, 128), term_ref.shape)
+    else:
+        grad_ref[0, share] = total
+
+
+def add_kernel(terms_ref, _, grad_ref):
+    total = jnp.sum(terms_ref[...], axis=0)
+    share = grad_ref.shape[1] - 1
+    for p in range(grad_ref.shape[0]):
+        grad_ref[p, share, 0:1] = total
+
+
+def end_kernel(back_ref, gradient_ref, loss_ref, sum_ref, sems):
+    peers, share, channels = back_ref.shape[0], back_ref.shape[1] - 1, gradient_ref.shape[0]
+    copies = []
+    for p in range(peers):
+        size = min(share, channels - p * share)
+        if size > 0:
+            copies.append(
+                pltpu.make_async_copy(
+                    back_ref.at[p, pl.ds(0, size)], gradient_ref.at[pl.ds(p * share, size)], sems.at[p]
+                )
+            )
+    for copy in copies:
+        copy.start()
+    total = back_ref[0, share, 0:1]
+    for p in range(1, peers):
+        total = total + back_ref[p, share, 0:1]
+    sum_ref[...] = jnp.broadcast_to(jnp.sum(total, axis=1, keepdims=True), sum_ref.shape)
+    copies.append(pltpu.make_async_copy(sum_ref, loss_ref, sems.at[peers]))
+    copies[-1].start()
+    for copy in copies:
+        copy.wait()
 
 
 def shards(members, target):
@@ -168,6 +201,10 @@
     apart = jnp.pad(members[0] - target, ((0, peers * share - channels), (0, 0), (0, 0)))
     own = spread(apart, PLANE, FIRST_PLANE).reshape(peers, share, row_count, col_count)
     vmem = pl.BlockSpec(memory_space=pltpu.VMEM)
+    shapes = [
+        jax.ShapeDtypeStruct((peers, share + 1, row_count, col_count), jnp.float32),
+        jax.ShapeDtypeStruct((lax.axis_size("z"), 1, col_count), jnp.float32),
+    ]
     grad = None
     halos = []
     start = 0
@@ -176,11 +213,11 @@
         halos.append((start, size, neighbour(part, 1), neighbour(part, -1)))
         start += size
     for start, size, west, east in halos:
-        grad = pl.pallas_call(
+        grad, *term = pl.pallas_call(
             functools.partial(box_kernel, loss_scale, grad_scale, channels, start, start + size == share),
-            out_shape=jax.ShapeDtypeStruct((peers, share + 1, row_count, col_count), jnp.float32),
+            out_shape=shapes if start + size == share else shapes[:1],
             in_specs=[vmem] * (4 if start == 0 else 5),
-            out_specs=vmem,
+            out_specs=[vmem] * (2 if start + size == share else 1),
             input_output_aliases={} if start == 0 else {4: 0},
             scratch_shapes=[
                 pltpu.VMEM((LEVELS + 1, bands, 8, 128), jnp.float32),
@@ -190,11 +227,30 @@
             compiler_params=pltpu.CompilerParams(vmem_limit_bytes=16 << 20),
             name=f"boxes_{start}",
         )(west, own, east, jnp.asarray(table), *(() if start == 0 else (grad,)))
+    terms = spread(term[0], ("z",), FIRST_Z)
+    grad = pl.pallas_call(
+        add_kernel,
+        out_shape=jax.ShapeDtypeStruct(grad.shape, jnp.float32),
+        in_specs=[vmem, vmem],
+        out_specs=vmem,
+        input_output_aliases={1: 0},
+        compiler_params=pltpu.CompilerParams(vmem_limit_bytes=4 << 20),
+        name="add_terms",
+    )(terms, grad)
     back = spread(grad, PLANE, FIRST_PLANE)
-    plane_loss = jnp.sum(back[:, share], axis=(0, 1))
-    all_loss = spread(jnp.broadcast_to(plane_loss, (lax.axis_size("z"), 1, col_count)), ("z",), FIRST_Z)
-    gradient = back[:, :share].reshape(1, peers * share, row_count, col_count)[:, :channels]
-    return gradient, jnp.sum(all_loss)
+    gradient, loss = pl.pallas_call(
+        end_kernel,
+        out_shape=(
+            jax.ShapeDtypeStruct((channels, row_count, col_count), jnp.float32),
+            jax.ShapeDtypeStruct((1, 128), jnp.float32),
+        ),
+        in_specs=[vmem],
+        out_specs=(pl.BlockSpec(memory_space=pl.ANY), pl.BlockSpec(memory_space=pl.ANY)),
+        scratch_shapes=[pltpu.VMEM((1, 128), jnp.float32), pltpu.SemaphoreType.DMA((peers + 1,))],
+        compiler_params=pltpu.CompilerParams(vmem_limit_bytes=4 << 20),
+        name="end",
+    )(back)
+    return gradient[None], loss[0, 0]
 
 
 def solution(mesh):

time: 67.1 us -> 66.5 us (level)
  blocking collectives: 33.7 us -> 48 us
  starting transfers between devices: 19.7 us -> 7.7 us
  waiting for transfers between devices: 5.02 us -> 3.35 us
  local copies, waits for them, and re-layouts: 1.45 us -> 0.06 us
  Pallas kernels: 4.15 us -> 5.04 us
    all_to_all x2 -> x3, blocking collectives: 33.7 us -> 48 us  [spread(): lax.all_to_all(value, axes, 0, 0, axis_index_groups=[order] if first else...]
    all_to_all x1 -> x0, starting transfers between devices: 12 us -> none  [spread(): lax.all_to_all(value, axes, 0, 0, axis_index_groups=[order] if first else...]
    all_to_all x1 -> x0, waiting for transfers between devices: 1.67 us -> none  [spread(): lax.all_to_all(value, axes, 0, 0, axis_index_groups=[order] if first else...]
    pallas_call x0 -> x2, Pallas kernels: none -> 0.89 us  [the longest x1 0.87 us: shards(): pl.pallas_call(end_kernel, out_shape=(jax.ShapeDtypeStruct((channels, row...]
    slice x2 -> x0, local copies, waits for them, and re-layouts: 0.78 us -> none  [shards(): back[:, :share].reshape(1, peers * share, row_count, col_count)]
  transfers between devices with their start and end apart: 5 -> 4, of which waited for: 3 -> 2; matrix products, arithmetic and copies ran while one was open for 1% -> 0% of each run, Pallas kernels for 6% -> 6%
where the time goes in v4:
time: 66.5 us; the launch traced here: 66 us
  blocking collectives  48 us (72%)
  starting transfers between devices  7.7 us (12%)
  Pallas kernels  5.04 us (8%)
  waiting for transfers between devices  3.35 us (5%)
  other arithmetic  1.13 us (2%)
  between operations  0.67 us (1%)
    all_to_all x3, blocking collectives, spread(): lax.all_to_all(value, axes, 0, 0, axis_index_groups=[order] if first else...  48 us
    ppermute x4, starting transfers between devices, neighbour(): return lax.ppermute(value, LON, pairs)  7.7 us
    pallas_call x2, Pallas kernels, shards(): pl.pallas_call(functools.partial(box_kernel, loss_scale, grad_scale, chan...  4.16 us
    ppermute x4, waiting for transfers between devices, neighbour(): return lax.ppermute(value, LON, pairs)  3.35 us
  transfers between devices with their start and end apart: 4, of which 2 were waited for; matrix products, arithmetic and copies ran while one was open for 0% of the time, Pallas kernels for 6%

profile of v4, /device:TPU:6, one launch (start us, length us, event | category | flops | bytes accessed | tf_op | source)
XLA Modules:
  0.0 66.0 jit_solution(7913652231373168078)
XLA Ops:
  0.6 1.1 %bitcast_subtract_fusion = f32[87,8,128]{2,1,0:T(8,128)S(1)} fusion(f32[87,8,128]{2,1,0:T(8,128)} %param.4, f32[1,87,8,128]{3,2,1,0:T(8,128)} %param.3), kind=kLoop, calls=%fused_computation | loop fusion | flops 89088 | bytes 1069056 | tf_op jit(solution)/shard_map/sub | solution.py:201
  1.8 16.7 %all_to_all.15 = f32[96,8,128]{2,1,0:T(8,128)S(1)} all-to-all(f32[96,8,128]{2,1,0:T(8,128)S(1)} %pad.4), channel_id=1, replica_groups={{448,480,0,32,64,96,128,160,192,224,256,288,320,352,384,416},{449,481,1..., dimensions={0} | all-to-all | bytes 786432 | tf_op jit(solution)/shard_map/all_to_all | solution.py:48
  18.5 0.0 copy-start
  18.5 4.7 %collective-permute-start.3 = (f32[16,3,8,128]{3,2,1,0:T(8,128)S(1)}, f32[16,3,8,128]{3,2,1,0:T(8,128)S(1)}, u32[]{:S(2)}, u32[]{:S(2)}) collective-permute-start(f32[16,3,8,128]{3,2,1,0:T(8,128)S(1)} %get-tuple-element.10), channel_id=1, source_target_pairs={{0,31},{1,0},{2,1},{3,2},{4,3},{5,4},{6,5},{7,6},{8,7},{9,8},{10,9... | collective-permute-start | bytes 589832 | tf_op jit(solution)/shard_map/ppermute | solution.py:38
  23.3 0.0 collective-permute-start.2
  23.3 3.0 %collective-permute-start.1 = (f32[16,3,8,128]{3,2,1,0:T(8,128)S(1)}, f32[16,3,8,128]{3,2,1,0:T(8,128)S(1)}, u32[]{:S(2)}, u32[]{:S(2)}) collective-permute-start(f32[16,3,8,128]{3,2,1,0:T(8,128)S(1)} %get-tuple-element.11), channel_id=1, source_target_pairs={{0,31},{1,0},{2,1},{3,2},{4,3},{5,4},{6,5},{7,6},{8,7},{9,8},{10,9... | collective-permute-start | bytes 589832 | tf_op jit(solution)/shard_map/ppermute | solution.py:38
  26.2 0.0 collective-permute-start
  26.2 0.2 collective-permute-done.3.east_ref
  26.5 3.1 %collective-permute-done.2.west_ref = f32[16,3,8,128]{3,2,1,0:T(8,128)S(1)} collective-permute-done((f32[16,3,8,128]{3,2,1,0:T(8,128)S(1)}, f32[16,3,8,128]{3,2,1,0:T(8,128)S(1)}, u32[]{:S(2)}, u32[]{:S(2)}) %collective-permute-start.2) | collective-permute-done | bytes 196640 | tf_op jit(solution)/shard_map/ppermute | solution.py:38
  29.6 0.0 copy-done
  29.6 4.0 %boxes_0.1.refs_0_ = f32[16,7,8,128]{3,2,1,0:T(8,128)S(1)} custom-call(f32[16,3,8,128]{3,2,1,0:T(8,128)S(1)} %collective-permute-done.2.west_ref, f32[16,6,8,128]{3,2,1,0:T(8,128)S(1)} %bitcast.7, f32[16,3,8,128]{3,2,1,0:T(8,128)S(1)} %collective-permute-done.3.east_ref, f32[8,8,128]{2,1,0:T(8,128)S(1)} %copy-done), custom_call_target="tpu_custom_call" | custom-call | tf_op jit(solution)/shard_map/boxes_0/pallas_call | solution.py:216
  33.5 0.0 collective-permute-done.1.east_ref
  33.5 0.0 collective-permute-done.west_ref
  33.6 0.2 boxes_3.1
  33.8 14.3 %all_to_all.16.terms_ref = f32[16,1,128]{2,1,0:T(1,128)S(1)} all-to-all(f32[16,1,128]{2,1,0:T(1,128)S(1)} %get-tuple-element.6), channel_id=1, replica_groups={{16,18,20,22,24,26,28,30,0,2,4,6,8,10,12,14},{17,19,21,23,25,27,29,31,1..., dimensions={0} | all-to-all | bytes 16384 | tf_op jit(solution)/shard_map/all_to_all | solution.py:48
  48.1 17.0 %all_to_all.17.back_ref = f32[16,7,8,128]{3,2,1,0:T(8,128)S(1)} all-to-all(f32[16,7,8,128]{3,2,1,0:T(8,128)S(1)} %add_terms.1), channel_id=1, replica_groups={{448,480,0,32,64,96,128,160,192,224,256,288,320,352,384,416},{449,481,1..., dimensions={0} | all-to-all | bytes 917504 | tf_op jit(solution)/shard_map/all_to_all | solution.py:48
  65.1 0.9 %end.1 = (f32[87,8,128]{2,1,0:T(8,128)}, f32[1,128]{1,0:T(1,128)}) custom-call(f32[16,7,8,128]{3,2,1,0:T(8,128)S(1)} %all_to_all.17.back_ref), custom_call_target="tpu_custom_call" | custom-call | tf_op jit(solution)/shard_map/end/pallas_call | solution.py:241
  (3 shorter events, 0.1 us)
Async XLA Ops:
  18.5 11.1 %copy-start = (f32[8,8,128]{2,1,0:T(8,128)S(1)}, f32[8,8,128]{2,1,0:T(8,128)}, u32[]{:S(2)}) copy-start(f32[8,8,128]{2,1,0:T(8,128)} %constant.5.clone.table_ref) | copy-start | bytes 98308
  18.5 7.9 %collective-permute-start.3 = (f32[16,3,8,128]{3,2,1,0:T(8,128)S(1)}, f32[16,3,8,128]{3,2,1,0:T(8,128)S(1)}, u32[]{:S(2)}, u32[]{:S(2)}) collective-permute-start(f32[16,3,8,128]{3,2,1,0:T(8,128)S(1)} %get-tuple-element.10), channel_id=1, source_target_pairs={{0,31},{1,0},{2,1},{3,2},{4,3},{5,4},{6,5},{7,6},{8,7},{9,8},{10,9... | collective-permute-start | bytes 589832 | tf_op jit(solution)/shard_map/ppermute | solution.py:38
  23.3 6.3 %collective-permute-start.2 = (f32[16,3,8,128]{3,2,1,0:T(8,128)S(1)}, f32[16,3,8,128]{3,2,1,0:T(8,128)S(1)}, u32[]{:S(2)}, u32[]{:S(2)}) collective-permute-start(f32[16,3,8,128]{3,2,1,0:T(8,128)S(1)} %get-tuple-element.10), channel_id=1, source_target_pairs={{0,1},{1,2},{2,3},{3,4},{4,5},{5,6},{6,7},{7,8},{8,9},{9,10},{10,1... | collective-permute-start | bytes 589832 | tf_op jit(solution)/shard_map/ppermute | solution.py:38
  23.3 10.3 %collective-permute-start.1 = (f32[16,3,8,128]{3,2,1,0:T(8,128)S(1)}, f32[16,3,8,128]{3,2,1,0:T(8,128)S(1)}, u32[]{:S(2)}, u32[]{:S(2)}) collective-permute-start(f32[16,3,8,128]{3,2,1,0:T(8,128)S(1)} %get-tuple-element.11), channel_id=1, source_target_pairs={{0,31},{1,0},{2,1},{3,2},{4,3},{5,4},{6,5},{7,6},{8,7},{9,8},{10,9... | collective-permute-start | bytes 589832 | tf_op jit(solution)/shard_map/ppermute | solution.py:38
  26.2 7.3 %collective-permute-start = (f32[16,3,8,128]{3,2,1,0:T(8,128)S(1)}, f32[16,3,8,128]{3,2,1,0:T(8,128)S(1)}, u32[]{:S(2)}, u32[]{:S(2)}) collective-permute-start(f32[16,3,8,128]{3,2,1,0:T(8,128)S(1)} %get-tuple-element.11), channel_id=1, source_target_pairs={{0,1},{1,2},{2,3},{3,4},{4,5},{5,6},{6,7},{7,8},{8,9},{9,10},{10,1... | collective-permute-start | bytes 589832 | tf_op jit(solution)/shard_map/ppermute | solution.py:38

commit v5 on v4

--- a/solution.py
+++ b/solution.py
@@ -11,7 +11,7 @@
 
 LEVELS = 7
 EPS = 0.05
-GROUPS = (3, 3)
+GROUPS = (4, 2)
 FIRST_PLANE = 14
 FIRST_Z = 8
 PLANE = ("mem", "lat")
@@ -77,24 +77,19 @@
         before = [zero] + rolled[:-1]
         return [field[b] + jnp.where(row >= reach, rolled[b], before[b]) for b in range(bands)]
 
-    def cols_ahead(west, own, east, reach, last):
-        out = ([], [], [])
-        for b in range(bands):
-            rw, ro, re = (pltpu.roll(tile, 128 - reach, 1) for tile in (west[b], own[b], east[b]))
-            out[0].append(west[b] + jnp.where(lane < 128 - reach, rw, ro))
-            out[1].append(own[b] + jnp.where(lane < 128 - reach, ro, re))
-            if not last:
-                out[2].append(east[b] + re)
-        return out
-
-    def cols_behind(west, own, reach, last):
-        out = ([], [])
-        for b in range(bands):
-            rw, ro = pltpu.roll(west[b], reach, 1), pltpu.roll(own[b], reach, 1)
-            if not last:
-                out[0].append(west[b] + rw)
-            out[1].append(own[b] + jnp.where(lane >= reach, ro, rw))
-        return out
+    def ahead(tile, beyond, reach):
+        mixed = tile if beyond is None else jnp.where(lane >= reach, tile, beyond)
+        return tile + pltpu.roll(mixed, 128 - reach, 1)
+
+    def behind(tile, before, reach):
+        mixed = tile if before is None else jnp.where(lane < 128 - reach, tile, before)
+        return tile + pltpu.roll(mixed, reach, 1)
+
+    def three(west, own, east, reach, last):
+        return ahead(west, own, reach), ahead(own, east, reach), None if last else ahead(east, None, reach)
+
+    def two(west, own, reach, last):
+        return None if last else behind(west, None, reach), behind(own, west, reach)
 
     def evaluate(scale, first, second, band, side):
         eps = eps_ref[scale, band]
@@ -116,17 +111,19 @@
                 ]
             )
         for scale in range(LEVELS + 1):
-            if scale:
-                reach = 2 ** (scale - 1)
-                for m in range(2):
-                    if reach < 8 * bands:
-                        fields[m] = [rows_ahead(field, reach) for field in fields[m]]
-                    fields[m] = cols_ahead(*fields[m], reach, scale == LEVELS)
-            part = None
-            for side in range(2):
-                for b in range(bands):
+            reach, part = 2**scale, None
+            if scale < LEVELS:
+                summed = [[rows_ahead(field, reach) if reach < 8 * bands else field for field in fields[m]] for m in range(2)]
+                ahead_of = [([], [], []), ([], [], [])]
+            for b in range(bands):
+                if scale < LEVELS:
+                    for m in range(2):
+                        for side, tile in enumerate(three(*(field[b] for field in summed[m]), reach, scale == LEVELS - 1)):
+                            ahead_of[m][side].append(tile)
+                for side in range(2):
                     term = evaluate(scale, fields[0][side][b], fields[1][side][b], b, side)
                     part = term if part is None else part + term
+            fields = ahead_of
             total = total + part * loss_scale[scale]
         for m in range(2):
             adjoint = [[cot_ref[LEVELS, m, side, b] for b in range(bands)] for side in range(2)]
@@ -134,7 +131,7 @@
                 reach = 2**level
                 if reach < 8 * bands:
                     adjoint = [rows_behind(field, reach) for field in adjoint]
-                west, own = cols_behind(*adjoint, reach, level == 0)
+                west, own = zip(*(two(adjoint[0][b], adjoint[1][b], reach, level == 0) for b in range(bands)))
                 if level:
                     west = [west[b] + cot_ref[level, m, 0, b] for b in range(bands)]
                 own = [own[b] + cot_ref[level, m, 1, b] for b in range(bands)]

time: 66.5 us -> 65.9 us (level)
  waiting for transfers between devices: 3.35 us -> 1.06 us
  blocking collectives: 48 us -> 49.5 us
    ppermute x4, waiting for transfers between devices: 3.35 us -> 1.06 us  [neighbour(): return lax.ppermute(value, LON, pairs)]
    all_to_all x3, blocking collectives: 48 us -> 49.5 us  [spread(): lax.all_to_all(value, axes, 0, 0, axis_index_groups=[order] if first else...]
  transfers between devices with their start and end apart: 4 -> 4, of which waited for: 2 -> 1; matrix products, arithmetic and copies ran while one was open for 0% -> 0% of each run, Pallas kernels for 6% -> 6%
where the time goes in v5:
time: 65.9 us; the launch traced here: 65.3 us
  blocking collectives  49.5 us (75%)
  starting transfers between devices  7.72 us (12%)
  Pallas kernels  5.06 us (8%)
  other arithmetic  1.13 us (2%)
  waiting for transfers between devices  1.06 us (2%)
  between operations  0.7 us (1%)
    all_to_all x3, blocking collectives, spread(): lax.all_to_all(value, axes, 0, 0, axis_index_groups=[order] if first else...  49.5 us
    ppermute x4, starting transfers between devices, neighbour(): return lax.ppermute(value, LON, pairs)  7.72 us
    pallas_call x2, Pallas kernels, shards(): pl.pallas_call(functools.partial(box_kernel, loss_scale, grad_scale, chan...  4.17 us
  transfers between devices with their start and end apart: 4, of which 1 were waited for; matrix products, arithmetic and copies ran while one was open for 0% of the time, Pallas kernels for 6%

profile of v5, /device:TPU:6, one launch (start us, length us, event | category | flops | bytes accessed | tf_op | source)
XLA Modules:
  0.0 65.3 jit_solution(5139685179595264307)
XLA Ops:
  0.6 1.1 %bitcast_subtract_fusion = f32[87,8,128]{2,1,0:T(8,128)S(1)} fusion(f32[87,8,128]{2,1,0:T(8,128)} %param.4, f32[1,87,8,128]{3,2,1,0:T(8,128)} %param.3), kind=kLoop, calls=%fused_computation | loop fusion | flops 89088 | bytes 1069056 | tf_op jit(solution)/shard_map/sub | solution.py:198
  1.8 16.7 %all_to_all.15 = f32[96,8,128]{2,1,0:T(8,128)S(1)} all-to-all(f32[96,8,128]{2,1,0:T(8,128)S(1)} %pad.4), channel_id=1, replica_groups={{448,480,0,32,64,96,128,160,192,224,256,288,320,352,384,416},{449,481,1..., dimensions={0} | all-to-all | bytes 786432 | tf_op jit(solution)/shard_map/all_to_all | solution.py:48
  18.5 0.0 copy-start
  18.5 0.0 collective-permute-start.2
  18.6 4.7 %collective-permute-start.3 = (f32[16,4,8,128]{3,2,1,0:T(8,128)S(1)}, f32[16,4,8,128]{3,2,1,0:T(8,128)S(1)}, u32[]{:S(2)}, u32[]{:S(2)}) collective-permute-start(f32[16,4,8,128]{3,2,1,0:T(8,128)S(1)} %slice.13), channel_id=1, source_target_pairs={{0,31},{1,0},{2,1},{3,2},{4,3},{5,4},{6,5},{7,6},{8,7},{9,8},{10,9... | collective-permute-start | bytes 786440 | tf_op jit(solution)/shard_map/ppermute | solution.py:38
  23.3 0.0 collective-permute-start
  23.3 2.9 %collective-permute-start.1 = (f32[16,2,8,128]{3,2,1,0:T(8,128)S(1)}, f32[16,2,8,128]{3,2,1,0:T(8,128)S(1)}, u32[]{:S(2)}, u32[]{:S(2)}) collective-permute-start(f32[16,2,8,128]{3,2,1,0:T(8,128)S(1)} %slice.12), channel_id=1, source_target_pairs={{0,31},{1,0},{2,1},{3,2},{4,3},{5,4},{6,5},{7,6},{8,7},{9,8},{10,9... | collective-permute-start | bytes 393224 | tf_op jit(solution)/shard_map/ppermute | solution.py:38
  26.3 1.0 %collective-permute-done.2.west_ref = f32[16,4,8,128]{3,2,1,0:T(8,128)S(1)} collective-permute-done((f32[16,4,8,128]{3,2,1,0:T(8,128)S(1)}, f32[16,4,8,128]{3,2,1,0:T(8,128)S(1)}, u32[]{:S(2)}, u32[]{:S(2)}) %collective-permute-start.2) | collective-permute-done | bytes 262176 | tf_op jit(solution)/shard_map/ppermute | solution.py:38
  27.3 0.0 collective-permute-done.3.east_ref
  27.3 0.0 copy-done
  27.3 4.0 %boxes_0.1.refs_0_ = f32[16,7,8,128]{3,2,1,0:T(8,128)S(1)} custom-call(f32[16,4,8,128]{3,2,1,0:T(8,128)S(1)} %collective-permute-done.2.west_ref, f32[16,6,8,128]{3,2,1,0:T(8,128)S(1)} %bitcast.8, f32[16,4,8,128]{3,2,1,0:T(8,128)S(1)} %collective-permute-done.3.east_ref, f32[8,8,128]{2,1,0:T(8,128)S(1)} %copy-done), custom_call_target="tpu_custom_call" | custom-call | tf_op jit(solution)/shard_map/boxes_0/pallas_call | solution.py:213
  31.3 0.0 collective-permute-done.west_ref
  31.3 0.0 collective-permute-done.1.east_ref
  31.3 0.2 boxes_4.1
  31.5 15.4 %all_to_all.16.terms_ref = f32[16,1,128]{2,1,0:T(1,128)S(1)} all-to-all(f32[16,1,128]{2,1,0:T(1,128)S(1)} %get-tuple-element.6), channel_id=1, replica_groups={{16,18,20,22,24,26,28,30,0,2,4,6,8,10,12,14},{17,19,21,23,25,27,29,31,1..., dimensions={0} | all-to-all | bytes 16384 | tf_op jit(solution)/shard_map/all_to_all | solution.py:48
  46.9 17.5 %all_to_all.17.back_ref = f32[16,7,8,128]{3,2,1,0:T(8,128)S(1)} all-to-all(f32[16,7,8,128]{3,2,1,0:T(8,128)S(1)} %add_terms.1), channel_id=1, replica_groups={{448,480,0,32,64,96,128,160,192,224,256,288,320,352,384,416},{449,481,1..., dimensions={0} | all-to-all | bytes 917504 | tf_op jit(solution)/shard_map/all_to_all | solution.py:48
  64.4 0.9 %end.1 = (f32[87,8,128]{2,1,0:T(8,128)}, f32[1,128]{1,0:T(1,128)}) custom-call(f32[16,7,8,128]{3,2,1,0:T(8,128)S(1)} %all_to_all.17.back_ref), custom_call_target="tpu_custom_call" | custom-call | tf_op jit(solution)/shard_map/end/pallas_call | solution.py:238
  (4 shorter events, 0.1 us)
Async XLA Ops:
  18.5 8.8 %copy-start = (f32[8,8,128]{2,1,0:T(8,128)S(1)}, f32[8,8,128]{2,1,0:T(8,128)}, u32[]{:S(2)}) copy-start(f32[8,8,128]{2,1,0:T(8,128)} %constant.5.clone.table_ref) | copy-start | bytes 98308
  18.5 8.8 %collective-permute-start.2 = (f32[16,4,8,128]{3,2,1,0:T(8,128)S(1)}, f32[16,4,8,128]{3,2,1,0:T(8,128)S(1)}, u32[]{:S(2)}, u32[]{:S(2)}) collective-permute-start(f32[16,4,8,128]{3,2,1,0:T(8,128)S(1)} %slice.13), channel_id=1, source_target_pairs={{0,1},{1,2},{2,3},{3,4},{4,5},{5,6},{6,7},{7,8},{8,9},{9,10},{10,1... | collective-permute-start | bytes 786440 | tf_op jit(solution)/shard_map/ppermute | solution.py:38
  18.6 8.8 %collective-permute-start.3 = (f32[16,4,8,128]{3,2,1,0:T(8,128)S(1)}, f32[16,4,8,128]{3,2,1,0:T(8,128)S(1)}, u32[]{:S(2)}, u32[]{:S(2)}) collective-permute-start(f32[16,4,8,128]{3,2,1,0:T(8,128)S(1)} %slice.13), channel_id=1, source_target_pairs={{0,31},{1,0},{2,1},{3,2},{4,3},{5,4},{6,5},{7,6},{8,7},{9,8},{10,9... | collective-permute-start | bytes 786440 | tf_op jit(solution)/shard_map/ppermute | solution.py:38
  23.3 8.0 %collective-permute-start = (f32[16,2,8,128]{3,2,1,0:T(8,128)S(1)}, f32[16,2,8,128]{3,2,1,0:T(8,128)S(1)}, u32[]{:S(2)}, u32[]{:S(2)}) collective-permute-start(f32[16,2,8,128]{3,2,1,0:T(8,128)S(1)} %slice.12), channel_id=1, source_target_pairs={{0,1},{1,2},{2,3},{3,4},{4,5},{5,6},{6,7},{7,8},{8,9},{9,10},{10,1... | collective-permute-start | bytes 393224 | tf_op jit(solution)/shard_map/ppermute | solution.py:38
  23.3 8.0 %collective-permute-start.1 = (f32[16,2,8,128]{3,2,1,0:T(8,128)S(1)}, f32[16,2,8,128]{3,2,1,0:T(8,128)S(1)}, u32[]{:S(2)}, u32[]{:S(2)}) collective-permute-start(f32[16,2,8,128]{3,2,1,0:T(8,128)S(1)} %slice.12), channel_id=1, source_target_pairs={{0,31},{1,0},{2,1},{3,2},{4,3},{5,4},{6,5},{7,6},{8,7},{9,8},{10,9... | collective-permute-start | bytes 393224 | tf_op jit(solution)/shard_map/ppermute | solution.py:38

commit v6 on v5

--- a/solution.py
+++ b/solution.py
@@ -11,7 +11,7 @@
 
 LEVELS = 7
 EPS = 0.05
-GROUPS = (4, 2)
+GROUPS = (6,)
 FIRST_PLANE = 14
 FIRST_Z = 8
 PLANE = ("mem", "lat")

time: 65.9 us -> 68.5 us (1.039)
  waiting for transfers between devices: 1.06 us -> 8.41 us
  starting transfers between devices: 7.72 us -> 4.73 us
  blocking collectives: 49.5 us -> 48 us
    ppermute x4 -> x2, waiting for transfers between devices: 1.06 us -> 8.41 us  [neighbour(): return lax.ppermute(value, LON, pairs)]
    ppermute x4 -> x2, starting transfers between devices: 7.72 us -> 4.73 us  [neighbour(): return lax.ppermute(value, LON, pairs)]
    all_to_all x3, blocking collectives: 49.5 us -> 48 us  [spread(): lax.all_to_all(value, axes, 0, 0, axis_index_groups=[order] if first else...]
    pallas_call x2 -> x1, Pallas kernels: 4.17 us -> 3.98 us  [shards(): pl.pallas_call(functools.partial(box_kernel, loss_scale, grad_scale, chan...]
  transfers between devices with their start and end apart: 4 -> 2, of which waited for: 1 -> 2; matrix products, arithmetic and copies ran while one was open for 0% -> 0% of each run, Pallas kernels for 6% -> 0%
where the time goes in v6:
time: 68.5 us; the launch traced here: 67.8 us
  blocking collectives  48 us (70%)
  waiting for transfers between devices  8.41 us (12%)
  Pallas kernels  4.87 us (7%)
  starting transfers between devices  4.73 us (7%)
  other arithmetic  1.13 us (2%)
    all_to_all x3, blocking collectives, spread(): lax.all_to_all(value, axes, 0, 0, axis_index_groups=[order] if first else...  48 us
    ppermute x2, waiting for transfers between devices, neighbour(): return lax.ppermute(value, LON, pairs)  8.41 us
    ppermute x2, starting transfers between devices, neighbour(): return lax.ppermute(value, LON, pairs)  4.73 us
    pallas_call x1, Pallas kernels, shards(): pl.pallas_call(functools.partial(box_kernel, loss_scale, grad_scale, chan...  3.98 us
  transfers between devices with their start and end apart: 2, of which 2 were waited for; matrix products, arithmetic and copies ran while one was open for 0% of the time, Pallas kernels for 0%

profile of v6, /device:TPU:6, one launch (start us, length us, event | category | flops | bytes accessed | tf_op | source)
XLA Modules:
  0.0 67.8 jit_solution(12032836272363507766)
XLA Ops:
  0.6 1.1 %bitcast_subtract_fusion = f32[87,8,128]{2,1,0:T(8,128)S(1)} fusion(f32[87,8,128]{2,1,0:T(8,128)} %param.4, f32[1,87,8,128]{3,2,1,0:T(8,128)} %param.3), kind=kLoop, calls=%fused_computation | loop fusion | flops 89088 | bytes 1069056 | tf_op jit(solution)/shard_map/sub | solution.py:198
  1.8 0.0 copy-start
  1.8 16.7 %all_to_all.15 = f32[96,8,128]{2,1,0:T(8,128)S(1)} all-to-all(f32[96,8,128]{2,1,0:T(8,128)S(1)} %pad.4), channel_id=1, replica_groups={{448,480,0,32,64,96,128,160,192,224,256,288,320,352,384,416},{449,481,1..., dimensions={0} | all-to-all | bytes 786432 | tf_op jit(solution)/shard_map/all_to_all | solution.py:48
  18.5 4.7 %collective-permute-start.1 = (f32[16,6,8,128]{3,2,1,0:T(8,128)S(1)}, f32[16,6,8,128]{3,2,1,0:T(8,128)S(1)}, u32[]{:S(2)}, u32[]{:S(2)}) collective-permute-start(f32[16,6,8,128]{3,2,1,0:T(8,128)S(1)} %bitcast.6), channel_id=1, source_target_pairs={{0,31},{1,0},{2,1},{3,2},{4,3},{5,4},{6,5},{7,6},{8,7},{9,8},{10,9... | collective-permute-start | bytes 1179656 | tf_op jit(solution)/shard_map/ppermute | solution.py:38
  23.2 0.0 collective-permute-start
  23.2 5.3 %collective-permute-done.1.east_ref = f32[16,6,8,128]{3,2,1,0:T(8,128)S(1)} collective-permute-done((f32[16,6,8,128]{3,2,1,0:T(8,128)S(1)}, f32[16,6,8,128]{3,2,1,0:T(8,128)S(1)}, u32[]{:S(2)}, u32[]{:S(2)}) %collective-permute-start.1) | collective-permute-done | bytes 393248 | tf_op jit(solution)/shard_map/ppermute | solution.py:38
  28.5 3.1 %collective-permute-done.west_ref = f32[16,6,8,128]{3,2,1,0:T(8,128)S(1)} collective-permute-done((f32[16,6,8,128]{3,2,1,0:T(8,128)S(1)}, f32[16,6,8,128]{3,2,1,0:T(8,128)S(1)}, u32[]{:S(2)}, u32[]{:S(2)}) %collective-permute-start) | collective-permute-done | bytes 393248 | tf_op jit(solution)/shard_map/ppermute | solution.py:38
  31.6 0.0 copy-done
  31.6 4.0 %boxes_0.1 = (f32[16,7,8,128]{3,2,1,0:T(8,128)S(1)}, f32[16,1,128]{2,1,0:T(1,128)S(1)}) custom-call(f32[16,6,8,128]{3,2,1,0:T(8,128)S(1)} %collective-permute-done.west_ref, f32[16,6,8,128]{3,2,1,0:T(8,128)S(1)} %bitcast.8, f32[16,6,8,128]{3,2,1,0:T(8,128)S(1)} %collective-permute-done.1.east_ref, f32[8,8,128]{2,1,0:T(8,128)S(1)} %copy-done), custom_call_target="tpu_custom_call" | custom-call | tf_op jit(solution)/shard_map/boxes_0/pallas_call | solution.py:213
  35.6 14.3 %all_to_all.16.terms_ref = f32[16,1,128]{2,1,0:T(1,128)S(1)} all-to-all(f32[16,1,128]{2,1,0:T(1,128)S(1)} %get-tuple-element.6), channel_id=1, replica_groups={{16,18,20,22,24,26,28,30,0,2,4,6,8,10,12,14},{17,19,21,23,25,27,29,31,1..., dimensions={0} | all-to-all | bytes 16384 | tf_op jit(solution)/shard_map/all_to_all | solution.py:48
  49.9 17.0 %all_to_all.17.back_ref = f32[16,7,8,128]{3,2,1,0:T(8,128)S(1)} all-to-all(f32[16,7,8,128]{3,2,1,0:T(8,128)S(1)} %add_terms.1), channel_id=1, replica_groups={{448,480,0,32,64,96,128,160,192,224,256,288,320,352,384,416},{449,481,1..., dimensions={0} | all-to-all | bytes 917504 | tf_op jit(solution)/shard_map/all_to_all | solution.py:48
  67.0 0.9 %end.1 = (f32[87,8,128]{2,1,0:T(8,128)}, f32[1,128]{1,0:T(1,128)}) custom-call(f32[16,7,8,128]{3,2,1,0:T(8,128)S(1)} %all_to_all.17.back_ref), custom_call_target="tpu_custom_call" | custom-call | tf_op jit(solution)/shard_map/end/pallas_call | solution.py:238
  (2 shorter events, 0.1 us)
Async XLA Ops:
  1.8 29.9 %copy-start = (f32[8,8,128]{2,1,0:T(8,128)S(1)}, f32[8,8,128]{2,1,0:T(8,128)}, u32[]{:S(2)}) copy-start(f32[8,8,128]{2,1,0:T(8,128)} %constant.5.clone.table_ref) | copy-start | bytes 98308
  18.5 10.0 %collective-permute-start.1 = (f32[16,6,8,128]{3,2,1,0:T(8,128)S(1)}, f32[16,6,8,128]{3,2,1,0:T(8,128)S(1)}, u32[]{:S(2)}, u32[]{:S(2)}) collective-permute-start(f32[16,6,8,128]{3,2,1,0:T(8,128)S(1)} %bitcast.6), channel_id=1, source_target_pairs={{0,31},{1,0},{2,1},{3,2},{4,3},{5,4},{6,5},{7,6},{8,7},{9,8},{10,9... | collective-permute-start | bytes 1179656 | tf_op jit(solution)/shard_map/ppermute | solution.py:38
  23.2 8.4 %collective-permute-start = (f32[16,6,8,128]{3,2,1,0:T(8,128)S(1)}, f32[16,6,8,128]{3,2,1,0:T(8,128)S(1)}, u32[]{:S(2)}, u32[]{:S(2)}) collective-permute-start(f32[16,6,8,128]{3,2,1,0:T(8,128)S(1)} %bitcast.7), channel_id=1, source_target_pairs={{0,1},{1,2},{2,3},{3,4},{4,5},{5,6},{6,7},{7,8},{8,9},{9,10},{10,1... | collective-permute-start | bytes 1179656 | tf_op jit(solution)/shard_map/ppermute | solution.py:38
